TPU v7x, 256 devices: a whole 4x4x8 slice. The times are simulated.
256 devices in a mesh: tmpl: 32 (over z_lo, y, x), sta: 8 (over z_hi, core).
Axes of the slice: x: 4, y: 4, z: 8 (z_hi: 4, z_lo: 2; z = z_hi * 2 + z_lo), core: 2. Of those that a mesh axis runs over, the one named last changes fastest.
Arguments:
- records: float32 [152, 4096], P('sta', 'tmpl'), may hold values from -6 to 6
- templates: float32 [128, 152, 600], P('tmpl', 'sta'), may hold values from -6 to 6
- offsets: int32 [128, 152], P('tmpl', 'sta'), may hold values from 0 to 425
- available: int32 [128, 152], P('tmpl', 'sta'), may hold values 0 or 1
Outputs:
- detection: float32 [128, 3072], P('tmpl', 'sta')
All inputs are finite; a program needn't handle non-finite values. No bound on the sum of `available` on one device may be relied on, other than what follows from the above.
Results may differ from a plain program's by a relative error of at most 0.0066.
Values may be sent and summed in bfloat16 or wider, within the bound.
No kernel may reach another device: no remote copies, remote signals or barrier semaphores. Data moves between devices by JAX's collectives and lax.ppermute only.
A program may use at most 64 MiB of HBM per device.

v0:
```python
import jax
import jax.numpy as jnp
from jax import lax
from jax.sharding import PartitionSpec as P

OFFMAX = 425


def copy_for_each(array, axis):
    count = lax.axis_size(axis)
    return lax.all_to_all(
        jnp.broadcast_to(array[None], (count, *array.shape)), axis, 0, 0, tiled=True
    )


def laid_out(parts, dim):
    parts = jnp.moveaxis(parts, 0, dim)
    dims = parts.shape
    return parts.reshape(*dims[:dim], dims[dim] * dims[dim + 1], *dims[dim + 2 :])


def gather_directly(array, axis, dim):
    parts = copy_for_each(array, axis)
    return laid_out(parts, dim)


def gathered_total(array, axis):
    parts = lax.all_gather(array, axis)
    return parts.sum(axis=0)


def scale_from(running, squared, length, positions):
    first = running[:, length : length + positions] - running[:, :positions]
    second = squared[:, length : length + positions] - squared[:, :positions]
    energy = second - first * first / length
    return 1.0 / jnp.sqrt(energy + 1e-05)


def framed(records_low, count, width, step):
    pieces = width // step
    total = (count + pieces - 1) * step
    padded = jnp.pad(records_low, ((0, 0), (0, total - records_low.shape[1])))
    rows_cut = padded.reshape(records_low.shape[0], count + pieces - 1, step)
    frames = jnp.stack([rows_cut[:, piece : piece + count] for piece in range(pieces)], axis=2)
    return frames.reshape(records_low.shape[0], count, width)


def shifted_copies(centred_low, width, step):
    length = centred_low.shape[2]
    padded = jnp.pad(centred_low, ((0, 0), (0, 0), (0, width + 1 - length)))
    tiled = jnp.tile(padded, (1, 1, step))[:, :, : step * width]
    return tiled.reshape(centred_low.shape[0], centred_low.shape[1], step, width)


def pick_lags(values, starts, count):
    return jax.vmap(jax.vmap(lambda series, start: lax.dynamic_slice_in_dim(series, start, count)))(
        values, starts
    )


def shards(records, templates, offsets, available):
    channels_here = records.shape[0]
    block_len = records.shape[1]
    templ_here = templates.shape[0]
    length = templates.shape[2]
    total_len = block_len * lax.axis_size("tmpl")
    lag_count = total_len - OFFMAX - length + 1
    positions = lag_count + OFFMAX
    step = 32
    width = step * ((length + 2 * step - 2) // step)
    count = (positions + step - 1) // step
    anchor = jnp.zeros((channels_here, 1), jnp.float32)
    whole = gather_directly(records, "tmpl", 1)
    running = jnp.concatenate([anchor, jnp.cumsum(whole, axis=1)], axis=1)
    squared = jnp.concatenate([anchor, jnp.cumsum(whole * whole, axis=1)], axis=1)
    whole_low = whole.astype(jnp.bfloat16)
    scale = scale_from(running, squared, length, positions)
    scale = jnp.pad(scale, ((0, 0), (0, count * step - positions)))
    frames = framed(whole_low, count, width, step)
    group_size = min(4, templ_here)
    groups = templ_here // group_size

    def stack_group(inputs):
        shapes, starts, present = inputs
        centred = shapes - jnp.mean(shapes, axis=2, keepdims=True)
        norms = jnp.sqrt(jnp.sum(centred * centred, axis=2) + 1e-05)
        copies = shifted_copies(centred.astype(jnp.bfloat16), width, step)
        correlated = jnp.einsum(
            "tcsw,cbw->tcbs", copies, frames, preferred_element_type=jnp.float32
        )
        correlated = correlated.reshape(group_size, channels_here, count * step)
        picked = pick_lags(correlated * scale[None], starts, lag_count)
        return jnp.sum(picked * (present.astype(jnp.float32) / norms)[:, :, None], axis=1)

    partial_stack = lax.map(
        stack_group,
        (
            templates.reshape(groups, group_size, channels_here, length),
            offsets.reshape(groups, group_size, channels_here),
            available.reshape(groups, group_size, channels_here),
        ),
    )
    partial_stack = partial_stack.reshape(templ_here, lag_count)
    share = lag_count // lax.axis_size("sta")
    full_stack = gathered_total(partial_stack, "sta")
    power = jnp.mean(full_stack * full_stack, axis=1, keepdims=True)
    mine = lax.dynamic_slice_in_dim(full_stack, lax.axis_index("sta") * share, share, 1)
    return mine / jnp.sqrt(power + 1e-05)


def solution(mesh):
    in_specs = (P("sta", "tmpl"), P("tmpl", "sta", None), P("tmpl", "sta"), P("tmpl", "sta"))
    out_specs = P("tmpl", "sta")
    return jax.shard_map(shards, mesh=mesh, in_specs=in_specs, out_specs=out_specs, check_vma=False)
```

profile of v0, /device:TPU:1, one launch (start us, length us, event | category | flops | bytes accessed | tf_op | source)
XLA Modules:
  0.0 363.0 jit_solution(13920081915653025096)
XLA Ops:
  1.5 9.2 %all-to-all-start = ((f32[32,19,128]{2,1,0:T(8,128)}), f32[32,19,128]{2,1,0:T(8,128)S(1)}, u32[]{:S(2)}, u32[]{:S(2)}) async-start(f32[32,19,128]{2,1,0:T(8,128)} %broadcast_in_dim.23), calls=%async_computation | async-start | bytes 786432 | tf_op jit(solution)/shard_map/all_to_all | solution.py:11
  13.0 2.1 tile.14
  15.0 8.4 %tile.15 = bf16[4,19,20512]{2,0,1:T(4,128)(2,1)S(1)} reshape(bf16[4,19,32,641]{3,2,0,1:T(8,128)(2,1)} %tile.14) | data formatting | bytes 6235648 | tf_op jit(solution)/shard_map/while/body/eval_jaxpr/tile | solution.py:51
  23.4 3.2 slice.150
  26.6 7.5 %reshape.69 = bf16[4,19,32,640]{3,2,0,1:T(8,128)(2,1)} reshape(bf16[4,19,20480]{2,0,1:T(4,128)(2,1)} %slice.150) | data formatting | bytes 6225920 | tf_op jit(solution)/shard_map/while/body/eval_jaxpr/reshape | solution.py:52
  35.7 5.0 %fusion.10 = (bf16[19,110,32]{2,1,0:T(8,128)(2,1)}, bf16[19,110,1,32]{3,1,0,2:T(8,128)(2,1)}, bf16[19,110,1,32]{3,1,0,2:T(8,128)(2,1)}, bf16[19,110,1,32]{3,1,0,...) fusion(bf16[19,129,32]{2,1,0:T(8,128)(2,1)S(1)} %reshape.67), kind=kLoop, calls=%fused_computation.70 | loop fusion | bytes 5082880 | tf_op jit(solution)/shard_map/slice | solution.py:44
  40.7 5.5 %reduce-window.16 = f32[19,32,128]{2,1,0:T(8,128)S(1)} reduce-window(f32[19,32,128]{2,1,0:T(8,128)S(1)} %get-tuple-element.59, f32[]{:T(128)} %constant.21.clone.1), window={size=1x1x128 pad=0_0x0_0x127_0}, to_apply=%region_3.4 | reduce-window | flops 9883648 | bytes 622596 | tf_op jit(solution)/shard_map/reduce-window.2
  99.3 2.9 convolution_bitcast_fusion
  102.2 2.9 copy.107
  105.1 3.6 %reshape.70 = f32[4,19,3520]{2,0,1:T(4,128)S(1)} reshape(f32[4,19,110,32]{3,2,0,1:T(8,128)} %copy.107) | data formatting | bytes 2140160 | tf_op jit(solution)/shard_map/while/body/eval_jaxpr/reshape | solution.py:91
  109.6 5.5 %reduce-window.14 = f32[19,32,128]{2,1,0:T(8,128)S(1)} reduce-window(f32[19,32,128]{2,1,0:T(8,128)S(1)} %copy-done.2, f32[]{:T(128)} %constant.21.clone.1), window={size=1x1x128 pad=0_0x0_0x127_0}, to_apply=%region_1.2 | reduce-window | flops 9883648 | bytes 622596 | tf_op jit(solution)/shard_map/reduce-window
  117.0 226.5 %while.1 = (s32[]{:T(128)}, f32[4,19,3520]{2,0,1:T(4,128)S(1)}, s32[76,3]{0,1:T(4,128)S(1)}, f32[76,3072]{1,0:T(8,128)S(1)}, s32[]{:T(128)}, /*index=5*/s32[]{:T(128)}) while((s32[]{:T(128)}, f32[4,19,3520]{2,0,1:T(4,128)S(1)}, s32[76,3]{0,1:T(4,128)S(1)}, f32[76,3072]{1,0:T(8,128)S(1)}, s32[]{:T(128)}, /*index=5*/s32[]{:T(128)}) %tuple.49), condition=%wide.while_cond, body=%wide.while_body.sunk | while | flops 2 | bytes 49289 | solution.py:56
  117.6 2.0 dynamic-slice_bitcast_fusion.2
  120.6 2.0 dynamic-slice_bitcast_fusion.2
  123.6 2.0 dynamic-slice_bitcast_fusion.2
  126.6 2.0 dynamic-slice_bitcast_fusion.2
  129.6 2.0 dynamic-slice_bitcast_fusion.2
  132.5 2.0 dynamic-slice_bitcast_fusion.2
  135.5 2.0 dynamic-slice_bitcast_fusion.2
  138.5 2.0 dynamic-slice_bitcast_fusion.2
  141.5 2.0 dynamic-slice_bitcast_fusion.2
  144.5 2.0 dynamic-slice_bitcast_fusion.2
  147.4 2.0 dynamic-slice_bitcast_fusion.2
  150.4 2.0 dynamic-slice_bitcast_fusion.2
  153.4 2.0 dynamic-slice_bitcast_fusion.2
  156.4 2.0 dynamic-slice_bitcast_fusion.2
  159.4 2.0 dynamic-slice_bitcast_fusion.2
  162.3 2.0 dynamic-slice_bitcast_fusion.2
  165.3 2.0 dynamic-slice_bitcast_fusion.2
  168.3 2.0 dynamic-slice_bitcast_fusion.2
  171.3 2.0 dynamic-slice_bitcast_fusion.2
  174.3 2.0 dynamic-slice_bitcast_fusion.2
  177.2 2.0 dynamic-slice_bitcast_fusion.2
  180.2 2.0 dynamic-slice_bitcast_fusion.2
  183.2 2.0 dynamic-slice_bitcast_fusion.2
  186.2 2.0 dynamic-slice_bitcast_fusion.2
  189.2 2.0 dynamic-slice_bitcast_fusion.2
  192.1 2.0 dynamic-slice_bitcast_fusion.2
  195.1 2.0 dynamic-slice_bitcast_fusion.2
  198.1 2.0 dynamic-slice_bitcast_fusion.2
  201.1 2.0 dynamic-slice_bitcast_fusion.2
  204.1 2.0 dynamic-slice_bitcast_fusion.2
  207.0 2.0 dynamic-slice_bitcast_fusion.2
  210.0 2.0 dynamic-slice_bitcast_fusion.2
  213.0 2.0 dynamic-slice_bitcast_fusion.2
  216.0 2.0 dynamic-slice_bitcast_fusion.2
  219.0 2.0 dynamic-slice_bitcast_fusion.2
  221.9 2.0 dynamic-slice_bitcast_fusion.2
  224.9 2.0 dynamic-slice_bitcast_fusion.2
  227.9 2.0 dynamic-slice_bitcast_fusion.2
  230.9 2.0 dynamic-slice_bitcast_fusion.2
  233.9 2.0 dynamic-slice_bitcast_fusion.2
  236.8 2.0 dynamic-slice_bitcast_fusion.2
  239.8 2.0 dynamic-slice_bitcast_fusion.2
  242.8 2.0 dynamic-slice_bitcast_fusion.2
  245.8 2.0 dynamic-slice_bitcast_fusion.2
  248.8 2.0 dynamic-slice_bitcast_fusion.2
  251.7 2.0 dynamic-slice_bitcast_fusion.2
  254.7 2.0 dynamic-slice_bitcast_fusion.2
  257.7 2.0 dynamic-slice_bitcast_fusion.2
  260.7 2.0 dynamic-slice_bitcast_fusion.2
  263.7 2.0 dynamic-slice_bitcast_fusion.2
  266.6 2.0 dynamic-slice_bitcast_fusion.2
  343.8 18.3 %all-gather.1 = f32[8,4,3072]{2,1,0:T(4,128)S(1)} all-gather(f32[1,4,3072]{2,1,0:T(4,128)S(1)} %bitcast.98), channel_id=2, replica_groups=mesh['tmpl'=32,'sta'=8] {'sta'}, dimensions={0}, use_global_device_ids=true | all-gather | bytes 442368 | tf_op jit(solution)/shard_map/all_gather | solution.py:28
  (355 shorter events, 185.5 us)
Async XLA Ops:
  1.5 32.8 %all-to-all-start = ((f32[32,19,128]{2,1,0:T(8,128)}), f32[32,19,128]{2,1,0:T(8,128)S(1)}, u32[]{:S(2)}, u32[]{:S(2)}) async-start(f32[32,19,128]{2,1,0:T(8,128)} %broadcast_in_dim.23), calls=%async_computation | async-start | bytes 786432 | tf_op jit(solution)/shard_map/all_to_all | solution.py:11
  26.6 7.5 %copy-start.10 = (s32[4,19]{1,0:T(4,128)S(1)}, s32[4,19]{1,0:T(4,128)}, u32[]{:S(2)}) copy-start(s32[4,19]{1,0:T(4,128)} %param.6) | copy-start | bytes 916
  26.6 7.7 %copy-start.9 = (s32[4,19]{1,0:T(4,128)S(1)}, s32[4,19]{1,0:T(4,128)}, u32[]{:S(2)}) copy-start(s32[4,19]{1,0:T(4,128)} %param.7) | copy-start | bytes 916
  83.8 13.6 %copy-start.8 = (bf16[19,110,1,32]{1,3,2,0:T(8,128)(2,1)S(1)}, bf16[19,110,1,32]{1,3,2,0:T(8,128)(2,1)}, u32[]{:S(2)}) copy-start(bf16[19,110,1,32]{1,3,2,0:T(8,128)(2,1)} %copy.102) | copy-start | bytes 401284
  83.8 13.6 %copy-start.7 = (bf16[19,110,1,32]{1,3,2,0:T(8,128)(2,1)S(1)}, bf16[19,110,1,32]{1,3,2,0:T(8,128)(2,1)}, u32[]{:S(2)}) copy-start(bf16[19,110,1,32]{1,3,2,0:T(8,128)(2,1)} %copy.103) | copy-start | bytes 401284
  83.8 13.6 %copy-start.6 = (bf16[19,110,1,32]{1,3,2,0:T(8,128)(2,1)S(1)}, bf16[19,110,1,32]{1,3,2,0:T(8,128)(2,1)}, u32[]{:S(2)}) copy-start(bf16[19,110,1,32]{1,3,2,0:T(8,128)(2,1)} %copy.104) | copy-start | bytes 401284
  83.8 13.7 %copy-start.4 = (bf16[19,110,1,32]{1,3,2,0:T(8,128)(2,1)S(1)}, bf16[19,110,1,32]{1,3,2,0:T(8,128)(2,1)}, u32[]{:S(2)}) copy-start(bf16[19,110,1,32]{1,3,2,0:T(8,128)(2,1)} %copy.105) | copy-start | bytes 401284
  83.8 13.7 %copy-start.5 = (bf16[19,110,32]{1,2,0:T(8,128)(2,1)S(1)}, bf16[19,110,32]{1,2,0:T(8,128)(2,1)}, u32[]{:S(2)}) copy-start(bf16[19,110,32]{1,2,0:T(8,128)(2,1)} %copy.86) | copy-start | bytes 401284
  83.9 15.4 %copy-start = (bf16[4,19,32,640]{3,2,0,1:T(8,128)(2,1)S(1)}, bf16[4,19,32,640]{3,2,0,1:T(8,128)(2,1)}, u32[]{:S(2)}) copy-start(bf16[4,19,32,640]{3,2,0,1:T(8,128)(2,1)} %reshape.69) | copy-start | bytes 9338884
  97.6 1.7 copy-start.1
  105.1 4.6 %copy-start.2 = (f32[19,32,128]{2,1,0:T(8,128)S(1)}, f32[19,32,128]{2,1,0:T(8,128)}, u32[]{:S(2)}) copy-start(f32[19,32,128]{2,1,0:T(8,128)} %get-tuple-element.58) | copy-start | bytes 933892
  115.8 1.2 copy-start.3
where the time goes:
time: 367 us; the launch traced here: 363 us
  local copies, waits for them, and re-layouts  313 us (85%)
  blocking collectives  18.3 us (5%)
  other arithmetic  16.5 us (4%)
  starting transfers between devices  9.21 us (3%)
    gather x304, local copies, waits for them, and re-layouts  224 us
    another operation x21, local copies, waits for them, and re-layouts, framed(): jnp.stack([rows_cut[:, piece:piece + count] for piece in range(pieces)],...  34.9 us
    all_gather x1, blocking collectives, gathered_total(): parts = lax.all_gather(array, axis)  18.3 us
    unnamed x49, local copies, waits for them, and re-layouts  17 us
    another operation x6, other arithmetic  11.6 us
    another operation x2, local copies, waits for them, and re-layouts, shifted_copies(): tiled = jnp.tile(padded, (1, 1, step))[:, :, :step * width]  10.4 us
    all_to_all x1, starting transfers between devices, copy_for_each(): lax.all_to_all(jnp.broadcast_to(array[None], (count, *array.shape)), axis...  9.21 us
    reshape x1, local copies, waits for them, and re-layouts, shifted_copies(): tiled.reshape(centred_low.shape[0], centred_low.shape[1], step, width)  7.45 us
  transfers between devices with their start and end apart: 1, of which 0 were waited for; matrix products, arithmetic and copies ran while one was open for 6% of the time, Pallas kernels for 0%

commit v1 on v0

v1 whole, which is shorter than its diff:
```python
import jax
import jax.numpy as jnp
from jax import lax
from jax.experimental import pallas as pl
from jax.experimental.pallas import tpu as pltpu
from jax.sharding import PartitionSpec as P

LANES = 128


def stack_kernel(off_ref, avail_ref, records_ref, templates_ref, out_ref, pad_ref, rev_ref, inv_ref, pieces_ref, sums_ref, moved_ref, acc_ref):
    templ_here, channels_here, length = templates_ref.shape
    blocks = records_ref.shape[0]
    taps = rev_ref.shape[2] // LANES
    lag_blocks = acc_ref.shape[1]
    bf16, f32 = jnp.bfloat16, jnp.float32

    row = lax.broadcasted_iota(jnp.int32, (LANES, LANES), 0)
    col = lax.broadcasted_iota(jnp.int32, (LANES, LANES), 1)
    flip = (row + col == LANES - 1).astype(f32).astype(bf16)
    pad_ref[...] = jnp.zeros_like(pad_ref)
    for t in range(templ_here):
        shapes = templates_ref[t]
        centred = shapes - jnp.sum(shapes, axis=1, keepdims=True) / length
        energy = jnp.sum(centred * centred, axis=1, keepdims=True)
        inv_ref[t] = jnp.broadcast_to(lax.rsqrt(energy + 1e-05), (channels_here, LANES))
        pad_ref[:, :length] = centred
        for q in range(taps):
            block = pad_ref[:, q * LANES : (q + 1) * LANES].astype(bf16)
            rev_ref[t, :, (taps - 1 - q) * LANES : (taps - q) * LANES] = jnp.dot(
                block, flip, preferred_element_type=f32
            )

    for c in range(channels_here):
        x = records_ref[:, c * LANES : (c + 1) * LANES]
        for k, v in enumerate((x, x * x)):
            rows = pl.ds((2 * c + k) * blocks, blocks)
            high = v.astype(bf16)
            rest = v - high.astype(f32)
            mid = rest.astype(bf16)
            low = (rest - mid.astype(f32)).astype(bf16)
            pieces_ref[rows, 0:LANES] = high
            pieces_ref[rows, LANES : 2 * LANES] = mid
            pieces_ref[rows, 2 * LANES : 3 * LANES] = low
    tail = (row >= col).astype(f32)
    adder = jnp.concatenate([tail, jnp.ones_like(tail)], axis=1).astype(bf16)
    adder = jnp.concatenate([adder, adder, adder], axis=0)
    sums = jnp.dot(pieces_ref[...], adder, preferred_element_type=f32)
    sums_ref[:, :blocks, :] = sums.reshape(2 * channels_here, blocks, 2 * LANES)
    sums_ref[:, blocks:, :] = jnp.zeros((2 * channels_here, sums_ref.shape[1] - blocks, 2 * LANES), f32)
    acc_ref[...] = jnp.zeros_like(acc_ref)

    whole = length // LANES
    left = length % LANES
    turn = LANES - left
    lane = lax.broadcasted_iota(jnp.int32, (blocks, LANES), 1)
    lag_lane = lax.broadcasted_iota(jnp.int32, (lag_blocks, LANES), 1)

    def window_sum(index):
        def at(i, k):
            return sums_ref[index, i : i + blocks, k * LANES : (k + 1) * LANES]

        total = at(0, 0)
        for i in range(1, whole + 1):
            total = total + at(i, 1)
        ends = jnp.where(lane < turn, 0.0, at(whole + 1, 1))
        near = pltpu.roll(at(whole, 0), turn, 1)
        far = pltpu.roll(at(whole + 1, 0), turn, 1)
        return total + (ends - jnp.where(lane < turn, near, far))

    def channel(c, carry):
        first = window_sum(2 * c)
        second = window_sum(2 * c + 1)
        scale = lax.rsqrt(second - first * first / length + 1e-05)

        x = records_ref[:, pl.ds(pl.multiple_of(c * LANES, LANES), LANES)]
        moved_ref[0, :blocks, :] = x
        moved_ref[0, blocks:, :] = jnp.zeros((moved_ref.shape[1] - blocks, LANES), f32)
        frames = jnp.concatenate(
            [moved_ref[0, q : q + blocks, :].astype(bf16) for q in range(taps)], axis=1
        )
        weights = []
        for t in range(templ_here):
            line = jnp.broadcast_to(rev_ref[t, pl.ds(c, 1), :], (LANES, taps * LANES))
            turned = pltpu.roll(line, (taps - 1) * LANES + 1, 1, stride=1, stride_axis=0).astype(bf16)
            weights.append(
                jnp.concatenate(
                    [turned[:, (taps - 1 - q) * LANES : (taps - q) * LANES] for q in range(taps)], axis=0
                )
            )
        correlated = jnp.dot(frames, jnp.concatenate(weights, axis=1), preferred_element_type=f32)
        for t in range(templ_here):
            start = off_ref[t, c]
            down = start // LANES
            over = start % LANES
            scaled = correlated[:, t * LANES : (t + 1) * LANES] * scale
            moved_ref[1 + t, :blocks, :] = pltpu.roll(scaled, (LANES - over) % LANES, 1)
            here = moved_ref[1 + t, pl.ds(down, lag_blocks), :]
            after = moved_ref[1 + t, pl.ds(down + 1, lag_blocks), :]
            picked = jnp.where(lag_lane < LANES - over, here, after)
            weight = inv_ref[t, pl.ds(c, 1), :] * avail_ref[t, c].astype(f32)
            acc_ref[t] += picked * weight
        return carry

    lax.fori_loop(0, channels_here, channel, 0)
    share = out_ref.shape[1] // templ_here
    for g in range(out_ref.shape[0]):
        for t in range(templ_here):
            out_ref[g, t * share : (t + 1) * share, :] = acc_ref[t, g * share : (g + 1) * share, :]


def partial_stacks(blocks, templates, offsets, available, lag_count, shares):
    count = blocks.shape[0]
    templ_here, channels_here, length = templates.shape
    taps = (length + 2 * LANES - 2) // LANES
    lag_blocks = lag_count // LANES
    f32 = jnp.float32
    smem = pl.BlockSpec(memory_space=pltpu.SMEM)
    vmem = pl.BlockSpec(memory_space=pltpu.VMEM)
    total_rows = 2 * channels_here * count
    return pl.pallas_call(
        stack_kernel,
        out_shape=jax.ShapeDtypeStruct((shares, templ_here * lag_blocks // shares, LANES), f32),
        in_specs=[smem, smem, vmem, vmem],
        out_specs=vmem,
        scratch_shapes=[
            pltpu.VMEM((channels_here, taps * LANES), f32),
            pltpu.VMEM((templ_here, channels_here, taps * LANES), f32),
            pltpu.VMEM((templ_here, channels_here, LANES), f32),
            pltpu.VMEM((total_rows, 3 * LANES), jnp.bfloat16),
            pltpu.VMEM((2 * channels_here, count + 8, 2 * LANES), f32),
            pltpu.VMEM((1 + templ_here, count + 8, LANES), f32),
            pltpu.VMEM((templ_here, lag_blocks, LANES), f32),
        ],
        compiler_params=pltpu.CompilerParams(vmem_limit_bytes=32 << 20),
        name="stack_channels",
    )(offsets, available, blocks, templates)


OFFMAX = 425


def shards(records, templates, offsets, available):
    channels_here, block_len = records.shape
    templ_here, _, length = templates.shape
    count = lax.axis_size("tmpl")
    shares = lax.axis_size("sta")
    lag_count = block_len * count - OFFMAX - length + 1
    mine = jnp.broadcast_to(records.reshape(1, channels_here * block_len), (count, channels_here * block_len))
    blocks = lax.all_to_all(mine, "tmpl", 0, 0, tiled=True)
    parts = partial_stacks(blocks, templates, offsets, available, lag_count, shares)
    parts = lax.all_to_all(parts, "sta", 0, 0, tiled=True)
    stack = jnp.sum(parts, axis=0).reshape(templ_here, lag_count // shares)
    power = lax.psum(jnp.sum(stack * stack, axis=1, keepdims=True), "sta") / lag_count
    return stack / jnp.sqrt(power + 1e-05)


def solution(mesh):
    in_specs = (P("sta", "tmpl"), P("tmpl", "sta", None), P("tmpl", "sta"), P("tmpl", "sta"))
    out_specs = P("tmpl", "sta")
    return jax.shard_map(shards, mesh=mesh, in_specs=in_specs, out_specs=out_specs, check_vma=False)
```

time: 367 us -> 64.7 us (0.18)
  local copies, waits for them, and re-layouts: 313 us -> 2.39 us
  other arithmetic: 16.5 us -> 0.93 us
  blocking collectives: 18.3 us -> 31.3 us
  Pallas kernels: 0 us -> 12 us
  waiting for transfers between devices: 0.01 us -> 8.33 us
    gather x306 -> x0, local copies, waits for them, and re-layouts: 224 us -> none
    another operation x25 -> x0, local copies, waits for them, and re-layouts: 45.9 us -> none  [the longest x21 34.9 us: framed(): jnp.stack([rows_cut[:, piece:piece + count] for piece in range(pieces)],...]
    all_gather x1 -> x0, blocking collectives: 18.3 us -> none  [gathered_total(): parts = lax.all_gather(array, axis)]
    all_to_all x0 -> x1, blocking collectives: none -> 17 us  [shards(): parts = lax.all_to_all(parts, 'sta', 0, 0, tiled=True)]
    unnamed x49 -> x8, local copies, waits for them, and re-layouts: 17 us -> 0.72 us
    psum x0 -> x1, blocking collectives: none -> 14.3 us  [shards(): lax.psum(jnp.sum(stack * stack, axis=1, keepdims=True), 'sta') / lag_count]
    pallas_call x0 -> x1, Pallas kernels: none -> 12 us  [partial_stacks(): pl.pallas_call(stack_kernel, out_shape=jax.ShapeDtypeStruct((shares, temp...]
    another operation x6 -> x0, other arithmetic: 11.6 us -> none
  transfers between devices with their start and end apart: 1 -> 1, of which waited for: 0 -> 1; matrix products, arithmetic and copies ran while one was open for 6% -> 0% of each run, Pallas kernels for 0% -> 0%
where the time goes in v1:
time: 64.7 us; the launch traced here: 64.3 us
  blocking collectives  31.3 us (48%)
  Pallas kernels  12 us (19%)
  starting transfers between devices  9.34 us (14%)
  waiting for transfers between devices  8.33 us (13%)
  local copies, waits for them, and re-layouts  2.39 us (4%)
  other arithmetic  0.93 us (1%)
    all_to_all x1, blocking collectives, shards(): parts = lax.all_to_all(parts, 'sta', 0, 0, tiled=True)  17 us
    psum x1, blocking collectives, shards(): lax.psum(jnp.sum(stack * stack, axis=1, keepdims=True), 'sta') / lag_count  14.3 us
    pallas_call x1, Pallas kernels, partial_stacks(): pl.pallas_call(stack_kernel, out_shape=jax.ShapeDtypeStruct((shares, temp...  12 us
    all_to_all x1, starting transfers between devices, shards(): blocks = lax.all_to_all(mine, 'tmpl', 0, 0, tiled=True)  9.34 us
    all_to_all x1, waiting for transfers between devices, shards(): blocks = lax.all_to_all(mine, 'tmpl', 0, 0, tiled=True)  8.33 us
    broadcast_in_dim x1, local copies, waits for them, and re-layouts, shards(): jnp.broadcast_to(records.reshape(1, channels_here * block_len), (count, c...  1.57 us
  transfers between devices with their start and end apart: 1, of which 1 were waited for; matrix products, arithmetic and copies ran while one was open for 0% of the time, Pallas kernels for 0%

profile of v1, /device:TPU:1, one launch (start us, length us, event | category | flops | bytes accessed | tf_op | source)
XLA Modules:
  0.0 64.3 jit_solution(16341714166490048046)
XLA Ops:
  0.0 1.6 %broadcast_in_dim.11 = f32[32,1,2432]{2,1,0:T(1,128)} broadcast(f32[2432]{0:T(1024)} %bitcast.8), dimensions={2} | broadcast | bytes 321024 | tf_op jit(solution)/shard_map/broadcast_in_dim | solution.py:149
  1.6 0.0 copy-start.2
  1.6 9.3 %all-to-all-start = ((f32[32,1,2432]{2,1,0:T(1,128)}), f32[32,1,2432]{2,1,0:T(1,128)S(1)}, u32[]{:S(2)}, u32[]{:S(2)}) async-start(f32[32,1,2432]{2,1,0:T(1,128)} %broadcast_in_dim.11), calls=%async_computation | async-start | bytes 622592 | tf_op jit(solution)/shard_map/all_to_all | solution.py:150
  10.9 0.0 copy-done.2
  11.0 8.3 %all-to-all-done = f32[32,1,2432]{2,1,0:T(1,128)S(1)} async-done(((f32[32,1,2432]{2,1,0:T(1,128)}), f32[32,1,2432]{2,1,0:T(1,128)S(1)}, u32[]{:S(2)}, u32[]{:S(2)}) %all-to-all-start) | async-done | bytes 311328 | tf_op jit(solution)/shard_map/all_to_all | solution.py:150
  19.3 0.0 copy-start
  19.3 0.0 copy-start.1
  19.3 0.7 %copy-done = s32[4,19]{1,0:T(4,128)S(1)} copy-done((s32[4,19]{1,0:T(4,128)S(1)}, s32[4,19]{1,0:T(4,128)}, u32[]{:S(2)}) %copy-start) | copy-done | bytes 328
  20.0 0.0 copy-done.1
  20.0 12.0 %stack_channels.1 = f32[8,12,128]{2,1,0:T(8,128)S(1)} custom-call(s32[4,19]{1,0:T(4,128)S(1)} %copy-done, s32[4,19]{1,0:T(4,128)S(1)} %copy-done.1, f32[32,2432]{1,0:T(8,128)S(1)} %bitcast.7, f32[4,19,600]{2,1,0:T(8,128)S(1)} %copy.6.templates_ref), custom_call_target="tpu_custom_call" | custom-call | tf_op jit(solution)/shard_map/stack_channels/pallas_call | solution.py:121
  32.0 17.0 %all_to_all.13 = f32[8,12,128]{2,1,0:T(8,128)S(1)} all-to-all(f32[8,12,128]{2,1,0:T(8,128)S(1)} %stack_channels.1), channel_id=1, replica_groups=mesh['tmpl'=32,'sta'=8] {'sta'}, dimensions={0} | all-to-all | bytes 98304 | tf_op jit(solution)/shard_map/all_to_all | solution.py:152
  49.0 0.1 multiply_reduce_fusion
  49.1 0.1 reduce_sum.27
  49.2 0.1 reduce_sum.28
  49.3 14.3 %psum.7 = f32[4,1]{0,1:T(1,128)S(1)} all-reduce(f32[4,1]{0,1:T(1,128)S(1)} %bitcast.9), channel_id=1, replica_groups=mesh['tmpl'=32,'sta'=8] {'sta'}, use_global_device_ids=true, to_apply=%region_3.4 | all-reduce | flops 4 | bytes 32 | tf_op jit(solution)/shard_map/psum | solution.py:154
  63.7 0.7 %broadcast_divide_fusion = f32[4,384]{1,0:T(4,128)} fusion(f32[4,384]{1,0:T(4,128)S(1)} %reshape.13, f32[4]{0:T(128)S(1)} %sqrt_bitcast_fusion), kind=kLoop, calls=%fused_computation.2 | loop fusion | flops 1536 | bytes 12304 | tf_op jit(solution)/shard_map/div | solution.py:155
  (5 shorter events, 0.1 us)
Async XLA Ops:
  1.6 9.4 %copy-start.2 = (f32[4,19,600]{2,0,1:T(4,128)S(1)}, f32[4,19,600]{2,0,1:T(4,128)}, u32[]{:S(2)}) copy-start(f32[4,19,600]{2,0,1:T(4,128)} %param.5) | copy-start | bytes 547204
  1.6 17.7 %all-to-all-start = ((f32[32,1,2432]{2,1,0:T(1,128)}), f32[32,1,2432]{2,1,0:T(1,128)S(1)}, u32[]{:S(2)}, u32[]{:S(2)}) async-start(f32[32,1,2432]{2,1,0:T(1,128)} %broadcast_in_dim.11), calls=%async_computation | async-start | bytes 622592 | tf_op jit(solution)/shard_map/all_to_all | solution.py:150
  19.3 0.7 %copy-start = (s32[4,19]{1,0:T(4,128)S(1)}, s32[4,19]{1,0:T(4,128)}, u32[]{:S(2)}) copy-start(s32[4,19]{1,0:T(4,128)} %off_ref.1) | copy-start | bytes 916
  19.3 0.7 %copy-start.1 = (s32[4,19]{1,0:T(4,128)S(1)}, s32[4,19]{1,0:T(4,128)}, u32[]{:S(2)}) copy-start(s32[4,19]{1,0:T(4,128)} %avail_ref.1) | copy-start | bytes 916

commit v2 on v1

v2 whole, which is shorter than its diff:
```python
import jax
import jax.numpy as jnp
from jax import lax
from jax.experimental import pallas as pl
from jax.experimental.pallas import tpu as pltpu
from jax.sharding import PartitionSpec as P

OFFMAX = 425
LANES = 128
SUBLANES = 8
SLOTS = 4
SMEM = pl.BlockSpec(memory_space=pltpu.SMEM)
VMEM = pl.BlockSpec(memory_space=pltpu.VMEM)
HBM = pl.BlockSpec(memory_space=pltpu.HBM)


def padded_rows(rows):
    return -(-rows // SUBLANES) * SUBLANES


def chunks_of(length, step):
    return (length + 2 * step - 2) // step


def limit(mib):
    return pltpu.CompilerParams(vmem_limit_bytes=mib << 20)


def spread_kernel(records_ref, out_ref, sem):
    channels = pl.ds(0, records_ref.shape[0])
    copies = [pltpu.make_async_copy(records_ref, out_ref.at[i, channels], sem.at[i]) for i in range(out_ref.shape[0])]
    for copy in copies:
        copy.start()
    for copy in copies:
        copy.wait()


def weights_kernel(templates_ref, weights_ref, inv_ref, lines_ref, chunks_ref):
    templ_here, channels_here, length = templates_ref.shape
    step = LANES // templ_here
    chunks = weights_ref.shape[1] // step
    groups = lines_ref.shape[0]
    width = templ_here * LANES
    bf16, f32 = jnp.bfloat16, jnp.float32
    lines_ref[...] = jnp.zeros_like(lines_ref)
    for t in range(templ_here):
        shapes = templates_ref[t]
        centred = shapes - jnp.sum(shapes, axis=1, keepdims=True) / length
        energy = jnp.sum(centred * centred, axis=1, keepdims=True)
        inv_ref[t] = jnp.broadcast_to(lax.rsqrt(energy + 1e-05), (channels_here, LANES))
        for q in range(groups):
            here = min(LANES, length - q * LANES)
            lines_ref[q, :channels_here, t * LANES : t * LANES + here] = centred[:, q * LANES : q * LANES + here]
    col = lax.broadcasted_iota(jnp.int32, (1, width), 1)
    source = LANES * ((col % LANES) // step) + step * (col // LANES) + step - 1 - col % step
    pick = (lax.broadcasted_iota(jnp.int32, (width, width), 0) == source).astype(f32).astype(bf16)
    lines = lines_ref[...].reshape(groups * lines_ref.shape[1], width).astype(bf16)
    picked = jnp.dot(lines, pick, preferred_element_type=f32)
    rows = lines_ref.shape[1]
    for m in range(chunks_ref.shape[0]):
        q, i = divmod(m, templ_here)
        chunks_ref[m] = picked[q * rows : (q + 1) * rows, i * LANES : (i + 1) * LANES]

    row = lax.broadcasted_iota(jnp.int32, (step, LANES), 0)
    inside = lax.broadcasted_iota(jnp.int32, (step, LANES), 1) % step <= row

    def channel(c, carry):
        before = jnp.zeros((step, LANES), f32)
        for m in range(chunks):
            if m * step < length:
                line = jnp.broadcast_to(chunks_ref[m, pl.ds(c, 1), :], (step, LANES))
                here = pltpu.roll(line, LANES - step + 1, 1, stride=1, stride_axis=0)
                following = pltpu.roll(line, 1, 1, stride=1, stride_axis=0)
            else:
                here = following = jnp.zeros((step, LANES), f32)
            weights_ref[c, m * step : (m + 1) * step, :] = jnp.where(inside, here, before).astype(bf16)
            before = following
        return carry

    lax.fori_loop(0, channels_here, channel, 0)


def stack_kernel(
    off_hbm, avail_hbm, records_ref, weights_ref, inv_ref, out_ref,
    off_ref, avail_ref, pieces_ref, sums_ref, framed_ref, moved_ref, acc_ref, sem,
    *, length,
):
    templ_here, channels_here, _ = inv_ref.shape
    step = LANES // templ_here
    blocks = framed_ref.shape[2] - SUBLANES
    pitch = records_ref.shape[0] // blocks
    lag_blocks = acc_ref.shape[1] // 2
    taps = weights_ref.shape[1] // LANES
    bf16, f32 = jnp.bfloat16, jnp.float32
    small = [pltpu.make_async_copy(off_hbm, off_ref, sem.at[0]), pltpu.make_async_copy(avail_hbm, avail_ref, sem.at[1])]
    for copy in small:
        copy.start()

    for c in range(channels_here):
        x = records_ref[pl.ds(c, blocks, stride=pitch), :]
        for k, v in enumerate((x, x * x)):
            rows = pl.ds((2 * c + k) * blocks, blocks)
            high = v.astype(bf16)
            rest = v - high.astype(f32)
            mid = rest.astype(bf16)
            low = (rest - mid.astype(f32)).astype(bf16)
            pieces_ref[rows, 0:LANES] = high
            pieces_ref[rows, LANES : 2 * LANES] = mid
            pieces_ref[rows, 2 * LANES : 3 * LANES] = low
    row = lax.broadcasted_iota(jnp.int32, (LANES, LANES), 0)
    col = lax.broadcasted_iota(jnp.int32, (LANES, LANES), 1)
    tail = (row >= col).astype(f32)
    adder = jnp.concatenate([tail, jnp.ones_like(tail)], axis=1).astype(bf16)
    adder = jnp.concatenate([adder, adder, adder], axis=0)
    sums = jnp.dot(pieces_ref[...], adder, preferred_element_type=f32)
    sums_ref[:, :blocks, :] = sums.reshape(2 * channels_here, blocks, 2 * LANES)
    sums_ref[:, blocks:, :] = jnp.zeros((2 * channels_here, SUBLANES, 2 * LANES), f32)
    acc_ref[...] = jnp.zeros_like(acc_ref)
    framed_ref[:, :, blocks:, :] = jnp.zeros((*framed_ref.shape[:2], SUBLANES, LANES), f32)
    for copy in small:
        copy.wait()

    whole = length // LANES
    turn = LANES - length % LANES
    lane = lax.broadcasted_iota(jnp.int32, (blocks, LANES), 1)
    lag_lane = lax.broadcasted_iota(jnp.int32, (lag_blocks, LANES), 1)

    def window_sum(index):
        def at(i, k):
            return sums_ref[index, i : i + blocks, k * LANES : (k + 1) * LANES]

        total = at(0, 0)
        for i in range(1, whole + 1):
            total = total + at(i, 1)
        ends = jnp.where(lane < turn, 0.0, at(whole + 1, 1))
        near = pltpu.roll(at(whole, 0), turn, 1)
        far = pltpu.roll(at(whole + 1, 0), turn, 1)
        return total + (ends - jnp.where(lane < turn, near, far))

    def regroup(arrays, group):
        count = len(arrays)
        distance = 1
        while distance < count:
            kept = (lane // group) // distance % 2 == 0
            swapped = list(arrays)
            for r in range(count):
                if r // distance % 2 == 0:
                    a, b = arrays[r], arrays[r + distance]
                    shift = group * distance
                    swapped[r] = jnp.where(kept, a, pltpu.roll(b, shift, 1))
                    swapped[r + distance] = jnp.where(kept, pltpu.roll(a, LANES - shift, 1), b)
            arrays = swapped
            distance *= 2
        return arrays

    for c in range(channels_here):
        slot = c % SLOTS
        first = window_sum(2 * c)
        second = window_sum(2 * c + 1)
        scale = lax.rsqrt(second - first * first / length + 1e-05)
        framed_ref[slot, 0, :blocks, :] = records_ref[pl.ds(c, blocks, stride=pitch), :]
        here = framed_ref[slot, 0, :blocks, :]
        after = framed_ref[slot, 0, 1 : blocks + 1, :]
        for r in range(1, templ_here):
            turned = LANES - r * step
            framed_ref[slot, r, :blocks, :] = jnp.where(
                lane < turned, pltpu.roll(here, turned, 1), pltpu.roll(after, turned, 1)
            )
        frames = jnp.concatenate(
            [
                jnp.concatenate([framed_ref[slot, r, q : q + blocks, :].astype(bf16) for q in range(taps)], axis=1)
                for r in range(templ_here)
            ],
            axis=0,
        )
        product = jnp.dot(frames, weights_ref[c], preferred_element_type=f32)
        correlated = regroup([product[r * blocks : (r + 1) * blocks, :] for r in range(templ_here)], step)
        for t in range(templ_here):
            start = off_ref[t, c]
            down = start // LANES
            over = start % LANES
            moved_ref[slot, t, :blocks, :] = pltpu.roll(correlated[t] * scale, (LANES - over) % LANES, 1)
            near = moved_ref[slot, t, pl.ds(down, lag_blocks), :]
            far = moved_ref[slot, t, pl.ds(down + 1, lag_blocks), :]
            picked = jnp.where(lag_lane < LANES - over, near, far)
            weight = inv_ref[t, c : c + 1, :] * avail_ref[t, c].astype(f32)
            acc_ref[t, :lag_blocks, :] += picked * weight

    shares = out_ref.shape[0]
    own = lag_blocks // shares
    for t in range(templ_here):
        acc_ref[t, lag_blocks:, :] = acc_ref[t, :lag_blocks, :]
        for g in range(shares):
            out_ref[g, t * lag_blocks : (t + 1) * lag_blocks, :] = acc_ref[
                t, g * own : g * own + lag_blocks, :
            ].astype(out_ref.dtype)


def finish_kernel(parts_ref, out_ref):
    templ_here, share = out_ref.shape
    lag_blocks = parts_ref.shape[1] // templ_here
    for t in range(templ_here):
        rows = pl.ds(t * lag_blocks, lag_blocks)
        stack = parts_ref[0, rows, :].astype(jnp.float32)
        for g in range(1, parts_ref.shape[0]):
            stack = stack + parts_ref[g, rows, :].astype(jnp.float32)
        power = jnp.sum(jnp.sum(stack * stack, axis=0, keepdims=True), axis=1, keepdims=True)
        unit = 1.0 / jnp.sqrt(power / (lag_blocks * LANES) + 1e-05)
        for i in range(share // LANES):
            out_ref[t : t + 1, i * LANES : (i + 1) * LANES] = stack[i : i + 1, :] * unit


def spread_records(records, count):
    rows = padded_rows(records.shape[0])
    return pl.pallas_call(
        spread_kernel,
        out_shape=jax.ShapeDtypeStruct((count, rows, records.shape[1]), records.dtype),
        in_specs=[HBM],
        out_specs=HBM,
        scratch_shapes=[pltpu.SemaphoreType.DMA((count,))],
        compiler_params=limit(1),
        name="spread_records",
    )(records)


def prepared_weights(templates):
    templ_here, channels_here, length = templates.shape
    step = LANES // templ_here
    groups = -(-length // LANES)
    rows = padded_rows(channels_here)
    lines = pltpu.VMEM((groups, rows, templ_here * LANES), jnp.float32)
    chunks = pltpu.VMEM((groups * templ_here, rows, LANES), jnp.float32)
    return pl.pallas_call(
        weights_kernel,
        out_shape=(
            jax.ShapeDtypeStruct((channels_here, chunks_of(length, step) * step, LANES), jnp.bfloat16),
            jax.ShapeDtypeStruct((templ_here, channels_here, LANES), jnp.float32),
        ),
        in_specs=[VMEM],
        out_specs=(VMEM, VMEM),
        scratch_shapes=[lines, chunks],
        compiler_params=limit(16),
        name="prepare_weights",
    )(templates)


def partial_stacks(blocks, count, weights, inv, offsets, available, lag_count, length, shares):
    templ_here, channels_here, _ = inv.shape
    lag_blocks = lag_count // LANES
    total_rows = 2 * channels_here * count
    f32 = jnp.float32
    return pl.pallas_call(
        lambda *refs: stack_kernel(*refs, length=length),
        out_shape=jax.ShapeDtypeStruct((shares, templ_here * lag_blocks, LANES), jnp.bfloat16),
        in_specs=[HBM, HBM, VMEM, VMEM, VMEM],
        out_specs=VMEM,
        scratch_shapes=[
            pltpu.SMEM(offsets.shape, offsets.dtype),
            pltpu.SMEM(available.shape, available.dtype),
            pltpu.VMEM((total_rows, 3 * LANES), jnp.bfloat16),
            pltpu.VMEM((2 * channels_here, count + SUBLANES, 2 * LANES), f32),
            pltpu.VMEM((SLOTS, templ_here, count + SUBLANES, LANES), f32),
            pltpu.VMEM((SLOTS, templ_here, count + SUBLANES, LANES), f32),
            pltpu.VMEM((templ_here, 2 * lag_blocks, LANES), f32),
            pltpu.SemaphoreType.DMA((2,)),
        ],
        compiler_params=limit(24),
        name="stack_channels",
    )(offsets, available, blocks, weights, inv)


def finished(parts, templ_here, share):
    return pl.pallas_call(
        finish_kernel,
        out_shape=jax.ShapeDtypeStruct((templ_here, share), jnp.float32),
        in_specs=[VMEM],
        out_specs=VMEM,
        compiler_params=limit(4),
        name="finish",
    )(parts)


def shards(records, templates, offsets, available):
    block_len = records.shape[1]
    templ_here, _, length = templates.shape
    count = lax.axis_size("tmpl")
    shares = lax.axis_size("sta")
    lag_count = block_len * count - OFFMAX - length + 1
    blocks = lax.all_to_all(spread_records(records, count), "tmpl", 0, 0, tiled=True)
    weights, inv = prepared_weights(templates)
    parts = partial_stacks(
        blocks.reshape(-1, block_len), count, weights, inv, offsets, available, lag_count, length, shares
    )
    parts = lax.all_to_all(parts, "sta", 0, 0, tiled=True)
    return finished(parts, templ_here, lag_count // shares)


def solution(mesh):
    in_specs = (P("sta", "tmpl"), P("tmpl", "sta", None), P("tmpl", "sta"), P("tmpl", "sta"))
    out_specs = P("tmpl", "sta")
    return jax.shard_map(shards, mesh=mesh, in_specs=in_specs, out_specs=out_specs, check_vma=False)
```

time: 64.7 us -> 45.1 us (0.70)
  blocking collectives: 31.3 us -> 18.5 us
  waiting for transfers between devices: 8.33 us -> 4.5 us
  Pallas kernels: 12 us -> 9.51 us
  other arithmetic: 0.93 us -> 0 us
    psum x1 -> x0, blocking collectives: 14.3 us -> none  [shards(): lax.psum(jnp.sum(stack * stack, axis=1, keepdims=True), 'sta') / lag_count]
    all_to_all x1, waiting for transfers between devices: 8.33 us -> 4.5 us  [shards(): lax.all_to_all(spread_records(records, count), 'tmpl', 0, 0, tiled=True)]
    pallas_call x1 -> x4, Pallas kernels: 12 us -> 9.51 us  [the longest x1 4.48 us: partial_stacks(): pl.pallas_call(lambda *refs: stack_kernel(*refs, length=length), out_shap...]
    unnamed x8 -> x7, local copies, waits for them, and re-layouts: 0.72 us -> 3.02 us
    broadcast_in_dim x1 -> x0, local copies, waits for them, and re-layouts: 1.57 us -> none  [shards(): jnp.broadcast_to(records.reshape(1, channels_here * block_len), (count, c...]
    all_to_all x1, blocking collectives: 17 us -> 18.5 us  [shards(): parts = lax.all_to_all(parts, 'sta', 0, 0, tiled=True)]
    div x2 -> x0, other arithmetic: 0.69 us -> none  [shards(): return stack / jnp.sqrt(power + 1e-05)]
  transfers between devices with their start and end apart: 1 -> 1, of which waited for: 1 -> 1; matrix products, arithmetic and copies ran while one was open for 0% -> 2% of each run, Pallas kernels for 0% -> 7%
where the time goes in v2:
time: 45.1 us; the launch traced here: 44.7 us
  blocking collectives  18.5 us (41%)
  Pallas kernels  9.51 us (21%)
  starting transfers between devices  9.23 us (20%)
  waiting for transfers between devices  4.5 us (10%)
  local copies, waits for them, and re-layouts  3.02 us (7%)
    all_to_all x1, blocking collectives, shards(): parts = lax.all_to_all(parts, 'sta', 0, 0, tiled=True)  18.5 us
    all_to_all x1, starting transfers between devices, shards(): lax.all_to_all(spread_records(records, count), 'tmpl', 0, 0, tiled=True)  9.23 us
    all_to_all x1, waiting for transfers between devices, shards(): lax.all_to_all(spread_records(records, count), 'tmpl', 0, 0, tiled=True)  4.5 us
    pallas_call x1, Pallas kernels, partial_stacks(): pl.pallas_call(lambda *refs: stack_kernel(*refs, length=length), out_shap...  4.48 us
    pallas_call x1, Pallas kernels, prepared_weights(): pl.pallas_call(weights_kernel, out_shape=(jax.ShapeDtypeStruct((channels_...  3.29 us
    unnamed x7, local copies, waits for them, and re-layouts  3.02 us
    pallas_call x1, Pallas kernels, spread_records(): pl.pallas_call(spread_kernel, out_shape=jax.ShapeDtypeStruct((count, rows...  1.02 us
  transfers between devices with their start and end apart: 1, of which 1 were waited for; matrix products, arithmetic and copies ran while one was open for 2% of the time, Pallas kernels for 7%

profile of v2, /device:TPU:1, one launch (start us, length us, event | category | flops | bytes accessed | tf_op | source)
XLA Modules:
  0.0 44.7 jit_solution(6545151739377738691)
XLA Ops:
  0.0 0.0 copy-start
  0.0 0.7 %copy-done = f32[19,128]{1,0:T(8,128)S(1)} copy-done((f32[19,128]{1,0:T(8,128)S(1)}, f32[19,128]{1,0:T(8,128)}, u32[]{:S(2)}) %copy-start) | copy-done | bytes 9752
  0.7 1.0 %spread_records.1 = f32[32,24,128]{2,1,0:T(8,128)} custom-call(f32[19,128]{1,0:T(8,128)S(1)} %copy-done), custom_call_target="tpu_custom_call" | custom-call | tf_op jit(solution)/shard_map/spread_records/pallas_call | solution.py:215
  1.7 9.2 %all-to-all-start = ((f32[32,24,128]{2,1,0:T(8,128)}), f32[32,24,128]{2,1,0:T(8,128)S(1)}, u32[]{:S(2)}, u32[]{:S(2)}) async-start(f32[32,24,128]{2,1,0:T(8,128)} %spread_records.1), calls=%async_computation | async-start | bytes 786432 | tf_op jit(solution)/shard_map/all_to_all | solution.py:289
  11.0 0.9 %copy.5.templates_ref = f32[4,19,600]{2,1,0:T(8,128)S(1)} copy(f32[4,19,600]{2,0,1:T(4,128)} %param.5) | data formatting | bytes 364800 | tf_op args[1]
  11.9 3.3 %prepare_weights.1 = (bf16[19,640,128]{2,1,0:T(8,128)(2,1)S(1)}, f32[4,19,128]{2,1,0:T(8,128)S(1)}) custom-call(f32[4,19,600]{2,1,0:T(8,128)S(1)} %copy.5.templates_ref), custom_call_target="tpu_custom_call" | custom-call | tf_op jit(solution)/shard_map/prepare_weights/pallas_call | solution.py:233
  15.2 4.5 %all-to-all-done = f32[32,24,128]{2,1,0:T(8,128)S(1)} async-done(((f32[32,24,128]{2,1,0:T(8,128)}), f32[32,24,128]{2,1,0:T(8,128)S(1)}, u32[]{:S(2)}, u32[]{:S(2)}) %all-to-all-start) | async-done | bytes 393248 | tf_op jit(solution)/shard_map/all_to_all | solution.py:289
  19.7 0.0 copy-start.1
  19.7 0.7 %copy-done.1 = s32[4,19]{1,0:T(4,128)S(1)} copy-done((s32[4,19]{1,0:T(4,128)S(1)}, s32[4,19]{1,0:T(4,128)}, u32[]{:S(2)}) %copy-start.1) | copy-done | bytes 328
  20.4 0.0 copy-start.2
  20.4 0.7 %copy-done.2 = s32[4,19]{1,0:T(4,128)S(1)} copy-done((s32[4,19]{1,0:T(4,128)S(1)}, s32[4,19]{1,0:T(4,128)}, u32[]{:S(2)}) %copy-start.2) | copy-done | bytes 328
  21.1 4.5 %stack_channels.1 = bf16[8,96,128]{2,1,0:T(8,128)(2,1)S(1)} custom-call(s32[4,19]{1,0:T(4,128)S(1)} %copy-done.1, s32[4,19]{1,0:T(4,128)S(1)} %copy-done.2, f32[768,128]{1,0:T(8,128)S(1)} %bitcast.1, bf16[19,640,128]{2,1,0:T(8,128)(2,1)S(1)} %get-tuple-element.7.refs_3_, f32[4,19,128]{2,1,0:T(8,128)S(1)} %get-tuple-element.8.refs_4_), custom_call_target="tpu_custom_call" | custom-call | tf_op jit(solution)/shard_map/stack_channels/pallas_call | solution.py:252
  25.6 18.5 %all_to_all.10.parts_ref = bf16[8,96,128]{2,1,0:T(8,128)(2,1)S(1)} all-to-all(bf16[8,96,128]{2,1,0:T(8,128)(2,1)S(1)} %stack_channels.1), channel_id=1, replica_groups=mesh['tmpl'=32,'sta'=8] {'sta'}, dimensions={0} | all-to-all | bytes 393216 | tf_op jit(solution)/shard_map/all_to_all | solution.py:294
  44.0 0.7 %finish.1 = f32[4,384]{1,0:T(4,128)} custom-call(bf16[8,96,128]{2,1,0:T(8,128)(2,1)S(1)} %all_to_all.10.parts_ref), custom_call_target="tpu_custom_call" | custom-call | tf_op jit(solution)/shard_map/finish/pallas_call | solution.py:273
Async XLA Ops:
  0.0 0.7 %copy-start = (f32[19,128]{1,0:T(8,128)S(1)}, f32[19,128]{1,0:T(8,128)}, u32[]{:S(2)}) copy-start(f32[19,128]{1,0:T(8,128)} %records_ref.1) | copy-start | bytes 29188
  1.7 18.0 %all-to-all-start = ((f32[32,24,128]{2,1,0:T(8,128)}), f32[32,24,128]{2,1,0:T(8,128)S(1)}, u32[]{:S(2)}, u32[]{:S(2)}) async-start(f32[32,24,128]{2,1,0:T(8,128)} %spread_records.1), calls=%async_computation | async-start | bytes 786432 | tf_op jit(solution)/shard_map/all_to_all | solution.py:289
  19.7 0.7 %copy-start.1 = (s32[4,19]{1,0:T(4,128)S(1)}, s32[4,19]{1,0:T(4,128)}, u32[]{:S(2)}) copy-start(s32[4,19]{1,0:T(4,128)} %refs_0_.1) | copy-start | bytes 916
  20.4 0.7 %copy-start.2 = (s32[4,19]{1,0:T(4,128)S(1)}, s32[4,19]{1,0:T(4,128)}, u32[]{:S(2)}) copy-start(s32[4,19]{1,0:T(4,128)} %refs_1_.1) | copy-start | bytes 916

commit v3 on v2

v3 whole, which is shorter than its diff:
```python
import jax
import jax.numpy as jnp
from jax import lax
from jax.experimental import pallas as pl
from jax.experimental.pallas import tpu as pltpu
from jax.sharding import PartitionSpec as P

OFFMAX = 425
LANES = 128
SUBLANES = 8
SLOTS = 4
SMEM = pl.BlockSpec(memory_space=pltpu.SMEM)
VMEM = pl.BlockSpec(memory_space=pltpu.VMEM)
HBM = pl.BlockSpec(memory_space=pltpu.HBM)


def padded_rows(rows):
    return -(-rows // SUBLANES) * SUBLANES


def chunks_of(length, step):
    return (length + 2 * step - 2) // step


def limit(mib):
    return pltpu.CompilerParams(vmem_limit_bytes=mib << 20)


def spread_kernel(records_ref, out_ref, tile_ref, sem):
    tile_ref[...] = jnp.zeros_like(tile_ref)
    tile_ref[: records_ref.shape[0], :] = records_ref[...]
    copies = [pltpu.make_async_copy(tile_ref, out_ref.at[i], sem.at[i]) for i in range(out_ref.shape[0])]
    for copy in copies:
        copy.start()
    for copy in copies:
        copy.wait()


def weights_kernel(templates_ref, weights_ref, inv_hbm, inv_ref, lines_ref, chunks_ref, sem):
    templ_here, channels_here, length = templates_ref.shape
    step = LANES // templ_here
    chunks = weights_ref.shape[1] // step
    groups = lines_ref.shape[0]
    width = templ_here * LANES
    bf16, f32 = jnp.bfloat16, jnp.float32
    lines_ref[...] = jnp.zeros_like(lines_ref)
    for t in range(templ_here):
        shapes = templates_ref[t]
        centred = shapes - jnp.sum(shapes, axis=1, keepdims=True) / length
        energy = jnp.sum(centred * centred, axis=1, keepdims=True)
        inv_ref[:, t * step : (t + 1) * step] = jnp.broadcast_to(lax.rsqrt(energy + 1e-05), (channels_here, step))
        for q in range(groups):
            here = min(LANES, length - q * LANES)
            lines_ref[q, :channels_here, t * LANES : t * LANES + here] = centred[:, q * LANES : q * LANES + here]
    inv_out = pltpu.make_async_copy(inv_ref, inv_hbm, sem)
    inv_out.start()
    col = lax.broadcasted_iota(jnp.int32, (1, width), 1)
    source = LANES * ((col % LANES) // step) + step * (col // LANES) + step - 1 - col % step
    pick = (lax.broadcasted_iota(jnp.int32, (width, width), 0) == source).astype(f32).astype(bf16)
    lines = lines_ref[...].reshape(groups * lines_ref.shape[1], width).astype(bf16)
    picked = jnp.dot(lines, pick, preferred_element_type=f32)
    rows = lines_ref.shape[1]
    for m in range(chunks_ref.shape[0]):
        q, i = divmod(m, templ_here)
        chunks_ref[m] = picked[q * rows : (q + 1) * rows, i * LANES : (i + 1) * LANES]

    row = lax.broadcasted_iota(jnp.int32, (step, LANES), 0)
    inside = lax.broadcasted_iota(jnp.int32, (step, LANES), 1) % step <= row

    for c in range(channels_here):
        before = jnp.zeros((step, LANES), f32)
        for m in range(chunks):
            if m * step < length:
                line = jnp.broadcast_to(chunks_ref[m, c : c + 1, :], (step, LANES))
                here = pltpu.roll(line, LANES - step + 1, 1, stride=1, stride_axis=0)
                following = pltpu.roll(line, 1, 1, stride=1, stride_axis=0)
            else:
                here = following = jnp.zeros((step, LANES), f32)
            weights_ref[c, m * step : (m + 1) * step, :] = jnp.where(inside, here, before).astype(bf16)
            before = following
    inv_out.wait()


def stack_kernel(
    off_hbm, avail_hbm, inv_hbm, records_ref, weights_ref, out_ref,
    off_ref, avail_ref, inv_ref, pieces_ref, tails_ref, totals_ref, acc_ref, sem, *slots,
    length,
):
    templ_here, channels_here = off_ref.shape
    step = LANES // templ_here
    blocks = tails_ref.shape[1] - SUBLANES
    framed = slots[: len(slots) // 2]
    moved = slots[len(slots) // 2 :]
    pitch = records_ref.shape[0] // blocks
    lag_blocks = acc_ref.shape[1]
    taps = weights_ref.shape[1] // LANES
    bf16, f32 = jnp.bfloat16, jnp.float32
    pairs = [(off_hbm, off_ref), (avail_hbm, avail_ref), (inv_hbm, inv_ref)]
    small = [pltpu.make_async_copy(*pair, sem.at[i]) for i, pair in enumerate(pairs)]
    for copy in small:
        copy.start()

    for c in range(channels_here):
        x = records_ref[pl.ds(c, blocks, stride=pitch), :]
        for k, v in enumerate((x, x * x)):
            rows = pl.ds((2 * c + k) * blocks, blocks)
            high = v.astype(bf16)
            rest = v - high.astype(f32)
            mid = rest.astype(bf16)
            low = (rest - mid.astype(f32)).astype(bf16)
            pieces_ref[rows, 0:LANES] = high
            pieces_ref[rows, LANES : 2 * LANES] = mid
            pieces_ref[rows, 2 * LANES : 3 * LANES] = low
    row = lax.broadcasted_iota(jnp.int32, (LANES, LANES), 0)
    col = lax.broadcasted_iota(jnp.int32, (LANES, LANES), 1)
    tail = (row >= col).astype(f32)
    adder = jnp.concatenate([tail, jnp.ones_like(tail)], axis=1).astype(bf16)
    adder = jnp.concatenate([adder, adder, adder], axis=0)
    sums = jnp.dot(pieces_ref[...], adder, preferred_element_type=f32)
    for k, ref in enumerate((tails_ref, totals_ref)):
        ref[:, :blocks, :] = sums[:, k * LANES : (k + 1) * LANES].reshape(2 * channels_here, blocks, LANES)
        ref[:, blocks:, :] = jnp.zeros((2 * channels_here, SUBLANES, LANES), f32)
    acc_ref[...] = jnp.zeros_like(acc_ref)
    for ref in framed:
        ref[blocks:, :] = jnp.zeros((SUBLANES, LANES), f32)
    for copy in small:
        copy.wait()

    whole = length // LANES
    turn = LANES - length % LANES
    lane = lax.broadcasted_iota(jnp.int32, (blocks, LANES), 1)
    lag_lane = lax.broadcasted_iota(jnp.int32, (lag_blocks, LANES), 1)

    def window_sum(index):
        def at(ref, i):
            return ref[index, i : i + blocks, :]

        total = at(tails_ref, 0)
        for i in range(1, whole + 1):
            total = total + at(totals_ref, i)
        ends = jnp.where(lane < turn, 0.0, at(totals_ref, whole + 1))
        near = pltpu.roll(at(tails_ref, whole), turn, 1)
        far = pltpu.roll(at(tails_ref, whole + 1), turn, 1)
        return total + (ends - jnp.where(lane < turn, near, far))

    def regroup(arrays, group):
        count = len(arrays)
        distance = 1
        while distance < count:
            kept = (lane // group) // distance % 2 == 0
            swapped = list(arrays)
            for r in range(count):
                if r // distance % 2 == 0:
                    a, b = arrays[r], arrays[r + distance]
                    shift = group * distance
                    swapped[r] = jnp.where(kept, a, pltpu.roll(b, shift, 1))
                    swapped[r + distance] = jnp.where(kept, pltpu.roll(a, LANES - shift, 1), b)
            arrays = swapped
            distance *= 2
        return arrays

    for c in range(channels_here):
        slot = c % SLOTS * templ_here
        first = window_sum(2 * c)
        second = window_sum(2 * c + 1)
        scale = lax.rsqrt(second - first * first / length + 1e-05)
        here = records_ref[pl.ds(c, blocks, stride=pitch), :]
        framed[slot][:blocks, :] = here
        for r in range(1, templ_here):
            ref = framed[slot + r]
            turned = pltpu.roll(here, LANES - r * step, 1)
            ref[:blocks, :] = turned
            ref[:blocks, :] = jnp.where(lane < LANES - r * step, turned, ref[1 : blocks + 1, :])
        frames = jnp.concatenate(
            [
                jnp.concatenate([framed[slot + r][q : q + blocks, :].astype(bf16) for q in range(taps)], axis=1)
                for r in range(templ_here)
            ],
            axis=0,
        )
        product = jnp.dot(frames, weights_ref[c], preferred_element_type=f32) * inv_ref[c : c + 1, :]
        correlated = regroup([product[r * blocks : (r + 1) * blocks, :] for r in range(templ_here)], step)
        for t in range(templ_here):
            start = off_ref[t, c]
            down = start // LANES
            over = start % LANES
            ref = moved[slot + t]
            ref[:blocks, :] = pltpu.roll(correlated[t] * scale, (LANES - over) % LANES, 1)
            near = ref[pl.ds(down, lag_blocks), :]
            far = ref[pl.ds(down + 1, lag_blocks), :]
            picked = jnp.where(lag_lane < LANES - over, near, far)
            acc_ref[t] += picked * avail_ref[t, c].astype(f32)

    for t in range(templ_here):
        out_ref[t * lag_blocks : (t + 1) * lag_blocks, :] = acc_ref[t]


def finish_kernel(place_ref, *refs):
    *parts, out_ref, stack_ref = refs
    templ_here, share = out_ref.shape
    lag_blocks = stack_ref.shape[0] // templ_here
    own = share // LANES
    for t in range(templ_here):
        rows = pl.ds(t * lag_blocks, lag_blocks)
        stack = parts[0][rows, :].astype(jnp.float32)
        for part in parts[1:]:
            stack = stack + part[rows, :].astype(jnp.float32)
        stack_ref[rows, :] = stack
        power = jnp.sum(jnp.sum(stack * stack, axis=0, keepdims=True), axis=1, keepdims=True)
        unit = 1.0 / jnp.sqrt(power / (lag_blocks * LANES) + 1e-05)
        for i in range(own):
            line = stack_ref[pl.ds(t * lag_blocks + place_ref[0] * own + i, 1), :]
            out_ref[t : t + 1, i * LANES : (i + 1) * LANES] = line * unit


def spread_records(records, count):
    rows = padded_rows(records.shape[0])
    return pl.pallas_call(
        spread_kernel,
        out_shape=jax.ShapeDtypeStruct((count, rows, records.shape[1]), records.dtype),
        in_specs=[VMEM],
        out_specs=HBM,
        scratch_shapes=[pltpu.VMEM((rows, records.shape[1]), records.dtype), pltpu.SemaphoreType.DMA((count,))],
        compiler_params=limit(1),
        name="spread_records",
    )(records)


def prepared_weights(templates):
    templ_here, channels_here, length = templates.shape
    step = LANES // templ_here
    groups = -(-length // LANES)
    rows = padded_rows(channels_here)
    lines = pltpu.VMEM((groups, rows, templ_here * LANES), jnp.float32)
    chunks = pltpu.VMEM((groups * templ_here, rows, LANES), jnp.float32)
    return pl.pallas_call(
        weights_kernel,
        out_shape=(
            jax.ShapeDtypeStruct((channels_here, chunks_of(length, step) * step, LANES), jnp.bfloat16),
            pltpu.HBM((channels_here, LANES), jnp.float32),
        ),
        in_specs=[VMEM],
        out_specs=(VMEM, HBM),
        scratch_shapes=[pltpu.VMEM((channels_here, LANES), jnp.float32), lines, chunks, pltpu.SemaphoreType.DMA(())],
        compiler_params=limit(16),
        name="prepare_weights",
    )(templates)


def partial_stacks(blocks, count, weights, inv, offsets, available, lag_count, length):
    templ_here, channels_here = offsets.shape
    offsets, available, inv = (pltpu.with_memory_space_constraint(a, pltpu.HBM) for a in (offsets, available, inv))
    lag_blocks = lag_count // LANES
    total_rows = 2 * channels_here * count
    f32 = jnp.float32
    return pl.pallas_call(
        lambda *refs: stack_kernel(*refs, length=length),
        out_shape=jax.ShapeDtypeStruct((templ_here * lag_blocks, LANES), f32),
        in_specs=[HBM, HBM, HBM, VMEM, VMEM],
        out_specs=VMEM,
        scratch_shapes=[
            pltpu.SMEM(offsets.shape, offsets.dtype),
            pltpu.SMEM(available.shape, available.dtype),
            pltpu.VMEM(inv.shape, f32),
            pltpu.VMEM((total_rows, 3 * LANES), jnp.bfloat16),
            pltpu.VMEM((2 * channels_here, count + SUBLANES, LANES), f32),
            pltpu.VMEM((2 * channels_here, count + SUBLANES, LANES), f32),
            pltpu.VMEM((templ_here, lag_blocks, LANES), f32),
            pltpu.SemaphoreType.DMA((3,)),
        ]
        + [pltpu.VMEM((count + SUBLANES, LANES), f32)] * (2 * SLOTS * templ_here),
        compiler_params=limit(24),
        name="stack_channels",
    )(offsets, available, inv, blocks, weights)


def finished(place, parts, templ_here, share):
    return pl.pallas_call(
        finish_kernel,
        out_shape=jax.ShapeDtypeStruct((templ_here, share), jnp.float32),
        in_specs=[SMEM] + [VMEM] * len(parts),
        out_specs=VMEM,
        scratch_shapes=[pltpu.VMEM(parts[0].shape, jnp.float32)],
        compiler_params=limit(4),
        name="finish",
    )(place, *parts)


MODE = "near_first"


def swapped(array, distance):
    return lax.ppermute(array, "sta", [(i, i ^ distance) for i in range(lax.axis_size("sta"))])


def shards(records, templates, offsets, available):
    block_len = records.shape[1]
    templ_here, _, length = templates.shape
    count = lax.axis_size("tmpl")
    shares = lax.axis_size("sta")
    lag_count = block_len * count - OFFMAX - length + 1
    blocks = lax.all_to_all(spread_records(records, count), "tmpl", 0, 0, tiled=True)
    weights, inv = prepared_weights(templates)
    mine = partial_stacks(blocks.reshape(-1, block_len), count, weights, inv, offsets, available, lag_count, length)
    place = lax.axis_index("sta").reshape(1).astype(jnp.int32)
    bf16 = jnp.bfloat16
    if MODE == "doubling":
        two = mine + swapped(mine, 1)
        four = two + swapped(two.astype(bf16), 2).astype(jnp.float32)
        parts = [four, swapped(four.astype(bf16), 4)]
    elif MODE == "core_last":
        low = mine.astype(bf16)
        four = mine + sum(swapped(low, d).astype(jnp.float32) for d in (2, 6, 4))
        parts = [four, swapped(four, 1)]
    else:
        theirs = swapped(mine, 1)
        low = (mine + theirs).astype(bf16)
        order = {"near_first": (2, 6, 4), "far_first": (4, 2, 6)}[MODE]
        parts = [mine, theirs] + [swapped(low, d) for d in order]
    return finished(place, parts, templ_here, lag_count // shares)


def solution(mesh):
    in_specs = (P("sta", "tmpl"), P("tmpl", "sta", None), P("tmpl", "sta"), P("tmpl", "sta"))
    out_specs = P("tmpl", "sta")
    return jax.shard_map(shards, mesh=mesh, in_specs=in_specs, out_specs=out_specs, check_vma=False)
```

time: 45.1 us -> 38.4 us (0.85)
  blocking collectives: 18.5 us -> 0 us
  starting transfers between devices: 9.23 us -> 19.1 us
  waiting for transfers between devices: 4.5 us -> 9.81 us
  Pallas kernels: 9.51 us -> 7.49 us
  local copies, waits for them, and re-layouts: 3.02 us -> 1.65 us
    all_to_all x1 -> x0, blocking collectives: 18.5 us -> none  [shards(): parts = lax.all_to_all(parts, 'sta', 0, 0, tiled=True)]
    ppermute x0 -> x4, starting transfers between devices: none -> 9.86 us  [swapped(): lax.ppermute(array, 'sta', [(i, i ^ distance) for i in range(lax.axis_siz...]
    ppermute x0 -> x4, waiting for transfers between devices: none -> 4.47 us  [swapped(): lax.ppermute(array, 'sta', [(i, i ^ distance) for i in range(lax.axis_siz...]
    unnamed x7 -> x3, local copies, waits for them, and re-layouts: 3.02 us -> 1.65 us
    pallas_call x1, Pallas kernels: 4.48 us -> 3.28 us  [partial_stacks(): pl.pallas_call(lambda *refs: stack_kernel(*refs, length=length), out_shap...]
    pallas_call x1, Pallas kernels: 3.29 us -> 2.45 us  [prepared_weights(): pl.pallas_call(weights_kernel, out_shape=(jax.ShapeDtypeStruct((channels_...]
    all_to_all x1, waiting for transfers between devices: 4.5 us -> 5.34 us  [shards(): lax.all_to_all(spread_records(records, count), 'tmpl', 0, 0, tiled=True)]
  transfers between devices with their start and end apart: 1 -> 5, of which waited for: 1 -> 3; matrix products, arithmetic and copies ran while one was open for 2% -> 2% of each run, Pallas kernels for 7% -> 6%
where the time goes in v3:
time: 38.4 us; the launch traced here: 38.1 us
  starting transfers between devices  19.1 us (50%)
  waiting for transfers between devices  9.81 us (26%)
  Pallas kernels  7.49 us (20%)
  local copies, waits for them, and re-layouts  1.65 us (4%)
    ppermute x4, starting transfers between devices, swapped(): lax.ppermute(array, 'sta', [(i, i ^ distance) for i in range(lax.axis_siz...  9.86 us
    all_to_all x1, starting transfers between devices, shards(): lax.all_to_all(spread_records(records, count), 'tmpl', 0, 0, tiled=True)  9.23 us
    all_to_all x1, waiting for transfers between devices, shards(): lax.all_to_all(spread_records(records, count), 'tmpl', 0, 0, tiled=True)  5.34 us
    ppermute x4, waiting for transfers between devices, swapped(): lax.ppermute(array, 'sta', [(i, i ^ distance) for i in range(lax.axis_siz...  4.47 us
    pallas_call x1, Pallas kernels, partial_stacks(): pl.pallas_call(lambda *refs: stack_kernel(*refs, length=length), out_shap...  3.28 us
    pallas_call x1, Pallas kernels, prepared_weights(): pl.pallas_call(weights_kernel, out_shape=(jax.ShapeDtypeStruct((channels_...  2.45 us
    unnamed x3, local copies, waits for them, and re-layouts  1.65 us
    pallas_call x1, Pallas kernels, spread_records(): pl.pallas_call(spread_kernel, out_shape=jax.ShapeDtypeStruct((count, rows...  1.04 us
  transfers between devices with their start and end apart: 5, of which 3 were waited for; matrix products, arithmetic and copies ran while one was open for 2% of the time, Pallas kernels for 6%

profile of v3, /device:TPU:1, one launch (start us, length us, event | category | flops | bytes accessed | tf_op | source)
XLA Modules:
  0.0 38.1 jit_solution(13995184795649444518)
XLA Ops:
  0.0 0.0 copy-start
  0.0 0.7 %copy-done = f32[19,128]{1,0:T(8,128)S(1)} copy-done((f32[19,128]{1,0:T(8,128)S(1)}, f32[19,128]{1,0:T(8,128)}, u32[]{:S(2)}) %copy-start) | copy-done | bytes 9752
  0.7 1.0 %spread_records.1 = f32[32,24,128]{2,1,0:T(8,128)} custom-call(f32[19,128]{1,0:T(8,128)S(1)} %copy-done), custom_call_target="tpu_custom_call" | custom-call | tf_op jit(solution)/shard_map/spread_records/pallas_call | solution.py:218
  1.8 9.2 %all-to-all-start = ((f32[32,24,128]{2,1,0:T(8,128)}), f32[32,24,128]{2,1,0:T(8,128)S(1)}, u32[]{:S(2)}, u32[]{:S(2)}) async-start(f32[32,24,128]{2,1,0:T(8,128)} %spread_records.1), calls=%async_computation | async-start | bytes 786432 | tf_op jit(solution)/shard_map/all_to_all | solution.py:302
  11.0 0.9 %copy.5.templates_ref = f32[4,19,600]{2,1,0:T(8,128)S(1)} copy(f32[4,19,600]{2,0,1:T(4,128)} %param.5) | data formatting | bytes 364800 | tf_op args[1]
  11.9 2.4 %prepare_weights.1 = (bf16[19,640,128]{2,1,0:T(8,128)(2,1)S(1)}, f32[19,128]{1,0:T(8,128)}) custom-call(f32[4,19,600]{2,1,0:T(8,128)S(1)} %copy.5.templates_ref), custom_call_target="tpu_custom_call" | custom-call | tf_op jit(solution)/shard_map/prepare_weights/pallas_call | solution.py:236
  14.4 5.3 %all-to-all-done = f32[32,24,128]{2,1,0:T(8,128)S(1)} async-done(((f32[32,24,128]{2,1,0:T(8,128)}), f32[32,24,128]{2,1,0:T(8,128)S(1)}, u32[]{:S(2)}, u32[]{:S(2)}) %all-to-all-start) | async-done | bytes 393248 | tf_op jit(solution)/shard_map/all_to_all | solution.py:302
  19.7 3.3 %stack_channels.1.refs_0_ = f32[96,128]{1,0:T(8,128)S(1)} custom-call(s32[4,19]{1,0:T(4,128)} %refs_0_.1, s32[4,19]{1,0:T(4,128)} %refs_1_.1, f32[19,128]{1,0:T(8,128)} %get-tuple-element.7.refs_2_, f32[768,128]{1,0:T(8,128)S(1)} %bitcast.2, bf16[19,640,128]{2,1,0:T(8,128)(2,1)S(1)} %get-tuple-element.8.refs_4_), custom_call_target="tpu_custom_call" | custom-call | tf_op jit(solution)/shard_map/stack_channels/pallas_call | solution.py:256
  23.0 2.6 %collective-permute-start = (f32[96,128]{1,0:T(8,128)S(1)}, f32[96,128]{1,0:T(8,128)S(1)}, u32[]{:S(2)}, u32[]{:S(2)}) collective-permute-start(f32[96,128]{1,0:T(8,128)S(1)} %stack_channels.1.refs_0_), channel_id=1, source_target_pairs={{0,1},{1,0},{2,3},{3,2},{4,5},{5,4},{6,7},{7,6},{8,9},{9,8},{10,11... | collective-permute-start | bytes 147464 | tf_op jit(solution)/shard_map/ppermute | solution.py:293
  25.6 0.9 %collective-permute-done.refs_1_ = f32[96,128]{1,0:T(8,128)S(1)} collective-permute-done((f32[96,128]{1,0:T(8,128)S(1)}, f32[96,128]{1,0:T(8,128)S(1)}, u32[]{:S(2)}, u32[]{:S(2)}) %collective-permute-start) | collective-permute-done | bytes 49184 | tf_op jit(solution)/shard_map/ppermute | solution.py:293
  26.5 6.1 %collective-permute-start.3 = (bf16[96,128]{1,0:T(8,128)(2,1)S(1)}, bf16[96,128]{1,0:T(8,128)(2,1)S(1)}, u32[]{:S(2)}, u32[]{:S(2)}) collective-permute-start(bf16[96,128]{1,0:T(8,128)(2,1)S(1)} %add_convert_fusion), channel_id=1, source_target_pairs={{0,4},{1,5},{2,6},{3,7},{4,0},{5,1},{6,2},{7,3},{8,12},{9,13},{10,... | collective-permute-start | bytes 73736 | tf_op jit(solution)/shard_map/ppermute | solution.py:293
  32.6 0.3 collective-permute-start.2
  32.9 0.9 %collective-permute-start.1 = (bf16[96,128]{1,0:T(8,128)(2,1)S(1)}, bf16[96,128]{1,0:T(8,128)(2,1)S(1)}, u32[]{:S(2)}, u32[]{:S(2)}) collective-permute-start(bf16[96,128]{1,0:T(8,128)(2,1)S(1)} %add_convert_fusion), channel_id=1, source_target_pairs={{0,2},{1,3},{2,0},{3,1},{4,6},{5,7},{6,4},{7,5},{8,10},{9,11},{10,... | collective-permute-start | bytes 73736 | tf_op jit(solution)/shard_map/ppermute | solution.py:293
  33.8 0.0 collective-permute-done.3.refs_4_
  33.8 3.6 %collective-permute-done.2.refs_3_ = bf16[96,128]{1,0:T(8,128)(2,1)S(1)} collective-permute-done((bf16[96,128]{1,0:T(8,128)(2,1)S(1)}, bf16[96,128]{1,0:T(8,128)(2,1)S(1)}, u32[]{:S(2)}, u32[]{:S(2)}) %collective-permute-start.2) | collective-permute-done | bytes 24608 | tf_op jit(solution)/shard_map/ppermute | solution.py:293
  37.4 0.0 collective-permute-done.1.refs_2_
  37.4 0.7 %finish.1 = f32[4,384]{1,0:T(4,128)} custom-call(s32[1]{0:T(128)} %bitcast.place_ref, f32[96,128]{1,0:T(8,128)S(1)} %stack_channels.1.refs_0_, f32[96,128]{1,0:T(8,128)S(1)} %collective-permute-done.refs_1_, bf16[96,128]{1,0:T(8,128)(2,1)S(1)} %collective-permute-done.1.refs_2_, bf16[96,128]{1,0:T(8,128)(2,1)S(1)} %collective-permute-done.2.refs_3_, ...), custom_call_target="tpu_custom_call" | custom-call | tf_op jit(solution)/shard_map/finish/pallas_call | solution.py:278
  (1 shorter events, 0.0 us)
Async XLA Ops:
  0.0 0.7 %copy-start = (f32[19,128]{1,0:T(8,128)S(1)}, f32[19,128]{1,0:T(8,128)}, u32[]{:S(2)}) copy-start(f32[19,128]{1,0:T(8,128)} %records_ref.1) | copy-start | bytes 29188
  1.8 18.0 %all-to-all-start = ((f32[32,24,128]{2,1,0:T(8,128)}), f32[32,24,128]{2,1,0:T(8,128)S(1)}, u32[]{:S(2)}, u32[]{:S(2)}) async-start(f32[32,24,128]{2,1,0:T(8,128)} %spread_records.1), calls=%async_computation | async-start | bytes 786432 | tf_op jit(solution)/shard_map/all_to_all | solution.py:302
  23.0 3.5 %collective-permute-start = (f32[96,128]{1,0:T(8,128)S(1)}, f32[96,128]{1,0:T(8,128)S(1)}, u32[]{:S(2)}, u32[]{:S(2)}) collective-permute-start(f32[96,128]{1,0:T(8,128)S(1)} %stack_channels.1.refs_0_), channel_id=1, source_target_pairs={{0,1},{1,0},{2,3},{3,2},{4,5},{5,4},{6,7},{7,6},{8,9},{9,8},{10,11... | collective-permute-start | bytes 147464 | tf_op jit(solution)/shard_map/ppermute | solution.py:293
  26.5 7.3 %collective-permute-start.3 = (bf16[96,128]{1,0:T(8,128)(2,1)S(1)}, bf16[96,128]{1,0:T(8,128)(2,1)S(1)}, u32[]{:S(2)}, u32[]{:S(2)}) collective-permute-start(bf16[96,128]{1,0:T(8,128)(2,1)S(1)} %add_convert_fusion), channel_id=1, source_target_pairs={{0,4},{1,5},{2,6},{3,7},{4,0},{5,1},{6,2},{7,3},{8,12},{9,13},{10,... | collective-permute-start | bytes 73736 | tf_op jit(solution)/shard_map/ppermute | solution.py:293
  32.6 4.8 %collective-permute-start.2 = (bf16[96,128]{1,0:T(8,128)(2,1)S(1)}, bf16[96,128]{1,0:T(8,128)(2,1)S(1)}, u32[]{:S(2)}, u32[]{:S(2)}) collective-permute-start(bf16[96,128]{1,0:T(8,128)(2,1)S(1)} %add_convert_fusion), channel_id=1, source_target_pairs={{0,6},{1,7},{2,4},{3,5},{4,2},{5,3},{6,0},{7,1},{8,14},{9,15},{10,... | collective-permute-start | bytes 73736 | tf_op jit(solution)/shard_map/ppermute | solution.py:293
  32.9 4.5 %collective-permute-start.1 = (bf16[96,128]{1,0:T(8,128)(2,1)S(1)}, bf16[96,128]{1,0:T(8,128)(2,1)S(1)}, u32[]{:S(2)}, u32[]{:S(2)}) collective-permute-start(bf16[96,128]{1,0:T(8,128)(2,1)S(1)} %add_convert_fusion), channel_id=1, source_target_pairs={{0,2},{1,3},{2,0},{3,1},{4,6},{5,7},{6,4},{7,5},{8,10},{9,11},{10,... | collective-permute-start | bytes 73736 | tf_op jit(solution)/shard_map/ppermute | solution.py:293

commit v4 on v3

--- a/solution.py
+++ b/solution.py
@@ -8,7 +8,6 @@
 OFFMAX = 425
 LANES = 128
 SUBLANES = 8
-SLOTS = 4
 SMEM = pl.BlockSpec(memory_space=pltpu.SMEM)
 VMEM = pl.BlockSpec(memory_space=pltpu.VMEM)
 HBM = pl.BlockSpec(memory_space=pltpu.HBM)
@@ -83,7 +82,7 @@
 
 def stack_kernel(
     off_hbm, avail_hbm, inv_hbm, records_ref, weights_ref, out_ref,
-    off_ref, avail_ref, inv_ref, pieces_ref, tails_ref, totals_ref, acc_ref, sem, *slots,
+    off_ref, avail_ref, inv_ref, pieces_ref, tails_ref, totals_ref, heads_ref, sem, *slots,
     length,
 ):
     templ_here, channels_here = off_ref.shape
@@ -92,7 +91,7 @@
     framed = slots[: len(slots) // 2]
     moved = slots[len(slots) // 2 :]
     pitch = records_ref.shape[0] // blocks
-    lag_blocks = acc_ref.shape[1]
+    lag_blocks = out_ref.shape[0] // templ_here
     taps = weights_ref.shape[1] // LANES
     bf16, f32 = jnp.bfloat16, jnp.float32
     pairs = [(off_hbm, off_ref), (avail_hbm, avail_ref), (inv_hbm, inv_ref)]
@@ -100,34 +99,34 @@
     for copy in small:
         copy.start()
 
-    for c in range(channels_here):
-        x = records_ref[pl.ds(c, blocks, stride=pitch), :]
-        for k, v in enumerate((x, x * x)):
-            rows = pl.ds((2 * c + k) * blocks, blocks)
-            high = v.astype(bf16)
-            rest = v - high.astype(f32)
-            mid = rest.astype(bf16)
-            low = (rest - mid.astype(f32)).astype(bf16)
-            pieces_ref[rows, 0:LANES] = high
-            pieces_ref[rows, LANES : 2 * LANES] = mid
-            pieces_ref[rows, 2 * LANES : 3 * LANES] = low
     row = lax.broadcasted_iota(jnp.int32, (LANES, LANES), 0)
     col = lax.broadcasted_iota(jnp.int32, (LANES, LANES), 1)
-    tail = (row >= col).astype(f32)
-    adder = jnp.concatenate([tail, jnp.ones_like(tail)], axis=1).astype(bf16)
-    adder = jnp.concatenate([adder, adder, adder], axis=0)
-    sums = jnp.dot(pieces_ref[...], adder, preferred_element_type=f32)
-    for k, ref in enumerate((tails_ref, totals_ref)):
-        ref[:, :blocks, :] = sums[:, k * LANES : (k + 1) * LANES].reshape(2 * channels_here, blocks, LANES)
-        ref[:, blocks:, :] = jnp.zeros((2 * channels_here, SUBLANES, LANES), f32)
-    acc_ref[...] = jnp.zeros_like(acc_ref)
+    turn = LANES - length % LANES
+    kinds = (row >= col, row >= 0, row < (col - turn) % LANES)
+    adder = jnp.concatenate([kind.astype(f32) for kind in kinds], axis=1).astype(bf16)
+    adder = jnp.concatenate([adder, adder], axis=0)
+
+    def block_sums():
+        for c in range(channels_here):
+            x = records_ref[pl.ds(c, blocks, stride=pitch), :]
+            for k, v in enumerate((x, x * x)):
+                rows = pl.ds((2 * c + k) * blocks, blocks)
+                high = v.astype(bf16)
+                pieces_ref[rows, 0:LANES] = high
+                pieces_ref[rows, LANES : 2 * LANES] = (v - high.astype(f32)).astype(bf16)
+        sums = jnp.dot(pieces_ref[...], adder, preferred_element_type=f32)
+        count = 2 * channels_here
+        for k, ref in enumerate((tails_ref, totals_ref, heads_ref)):
+            ref[:, :blocks, :] = sums[:, k * LANES : (k + 1) * LANES].reshape(count, blocks, LANES)
+            ref[:, blocks:, :] = jnp.zeros((count, SUBLANES, LANES), f32)
+
+    stacks = [jnp.zeros((lag_blocks, LANES), f32) for _ in range(templ_here)]
     for ref in framed:
         ref[blocks:, :] = jnp.zeros((SUBLANES, LANES), f32)
     for copy in small:
         copy.wait()
 
     whole = length // LANES
-    turn = LANES - length % LANES
     lane = lax.broadcasted_iota(jnp.int32, (blocks, LANES), 1)
     lag_lane = lax.broadcasted_iota(jnp.int32, (lag_blocks, LANES), 1)
 
@@ -136,12 +135,10 @@
             return ref[index, i : i + blocks, :]
 
         total = at(tails_ref, 0)
-        for i in range(1, whole + 1):
+        for i in range(1, whole):
             total = total + at(totals_ref, i)
-        ends = jnp.where(lane < turn, 0.0, at(totals_ref, whole + 1))
-        near = pltpu.roll(at(tails_ref, whole), turn, 1)
-        far = pltpu.roll(at(tails_ref, whole + 1), turn, 1)
-        return total + (ends - jnp.where(lane < turn, near, far))
+        ends = jnp.where(lane < turn, at(heads_ref, whole), at(totals_ref, whole) + at(heads_ref, whole + 1))
+        return total + ends
 
     def regroup(arrays, group):
         count = len(arrays)
@@ -159,8 +156,9 @@
             distance *= 2
         return arrays
 
+    block_sums()
     for c in range(channels_here):
-        slot = c % SLOTS * templ_here
+        slot = c * templ_here
         first = window_sum(2 * c)
         second = window_sum(2 * c + 1)
         scale = lax.rsqrt(second - first * first / length + 1e-05)
@@ -189,10 +187,10 @@
             near = ref[pl.ds(down, lag_blocks), :]
             far = ref[pl.ds(down + 1, lag_blocks), :]
             picked = jnp.where(lag_lane < LANES - over, near, far)
-            acc_ref[t] += picked * avail_ref[t, c].astype(f32)
+            stacks[t] = stacks[t] + picked * avail_ref[t, c].astype(f32)
 
     for t in range(templ_here):
-        out_ref[t * lag_blocks : (t + 1) * lag_blocks, :] = acc_ref[t]
+        out_ref[t * lag_blocks : (t + 1) * lag_blocks, :] = stacks[t]
 
 
 def finish_kernel(place_ref, *refs):
@@ -262,13 +260,13 @@
             pltpu.SMEM(offsets.shape, offsets.dtype),
             pltpu.SMEM(available.shape, available.dtype),
             pltpu.VMEM(inv.shape, f32),
-            pltpu.VMEM((total_rows, 3 * LANES), jnp.bfloat16),
+            pltpu.VMEM((total_rows, 2 * LANES), jnp.bfloat16),
             pltpu.VMEM((2 * channels_here, count + SUBLANES, LANES), f32),
             pltpu.VMEM((2 * channels_here, count + SUBLANES, LANES), f32),
-            pltpu.VMEM((templ_here, lag_blocks, LANES), f32),
+            pltpu.VMEM((2 * channels_here, count + SUBLANES, LANES), f32),
             pltpu.SemaphoreType.DMA((3,)),
         ]
-        + [pltpu.VMEM((count + SUBLANES, LANES), f32)] * (2 * SLOTS * templ_here),
+        + [pltpu.VMEM((count + SUBLANES, LANES), f32)] * (2 * channels_here * templ_here),
         compiler_params=limit(24),
         name="stack_channels",
     )(offsets, available, inv, blocks, weights)
@@ -286,9 +284,6 @@
     )(place, *parts)
 
 
-MODE = "near_first"
-
-
 def swapped(array, distance):
     return lax.ppermute(array, "sta", [(i, i ^ distance) for i in range(lax.axis_size("sta"))])
 
@@ -303,20 +298,9 @@
     weights, inv = prepared_weights(templates)
     mine = partial_stacks(blocks.reshape(-1, block_len), count, weights, inv, offsets, available, lag_count, length)
     place = lax.axis_index("sta").reshape(1).astype(jnp.int32)
-    bf16 = jnp.bfloat16
-    if MODE == "doubling":
-        two = mine + swapped(mine, 1)
-        four = two + swapped(two.astype(bf16), 2).astype(jnp.float32)
-        parts = [four, swapped(four.astype(bf16), 4)]
-    elif MODE == "core_last":
-        low = mine.astype(bf16)
-        four = mine + sum(swapped(low, d).astype(jnp.float32) for d in (2, 6, 4))
-        parts = [four, swapped(four, 1)]
-    else:
-        theirs = swapped(mine, 1)
-        low = (mine + theirs).astype(bf16)
-        order = {"near_first": (2, 6, 4), "far_first": (4, 2, 6)}[MODE]
-        parts = [mine, theirs] + [swapped(low, d) for d in order]
+    theirs = swapped(mine, 1)
+    pair = (mine + theirs).astype(jnp.bfloat16)
+    parts = [mine, theirs] + [swapped(pair, distance) for distance in (2, 6, 4)]
     return finished(place, parts, templ_here, lag_count // shares)
 
 

time: 38.4 us -> 37.9 us (0.987)
  Pallas kernels: 7.49 us -> 6.98 us
    pallas_call x1, Pallas kernels: 3.28 us -> 2.77 us  [partial_stacks(): pl.pallas_call(lambda *refs: stack_kernel(*refs, length=length), out_shap...]
  transfers between devices with their start and end apart: 5 -> 5, of which waited for: 3 -> 3; matrix products, arithmetic and copies ran while one was open for 2% -> 3% of each run, Pallas kernels for 6% -> 7%
where the time goes in v4:
time: 37.9 us; the launch traced here: 37.6 us
  starting transfers between devices  19.1 us (50%)
  waiting for transfers between devices  9.81 us (26%)
  Pallas kernels  6.98 us (18%)
  local copies, waits for them, and re-layouts  1.65 us (4%)
    ppermute x4, starting transfers between devices, swapped(): lax.ppermute(array, 'sta', [(i, i ^ distance) for i in range(lax.axis_siz...  9.87 us
    all_to_all x1, starting transfers between devices, shards(): lax.all_to_all(spread_records(records, count), 'tmpl', 0, 0, tiled=True)  9.23 us
    all_to_all x1, waiting for transfers between devices, shards(): lax.all_to_all(spread_records(records, count), 'tmpl', 0, 0, tiled=True)  5.34 us
    ppermute x4, waiting for transfers between devices, swapped(): lax.ppermute(array, 'sta', [(i, i ^ distance) for i in range(lax.axis_siz...  4.47 us
    pallas_call x1, Pallas kernels, partial_stacks(): pl.pallas_call(lambda *refs: stack_kernel(*refs, length=length), out_shap...  2.77 us
    pallas_call x1, Pallas kernels, prepared_weights(): pl.pallas_call(weights_kernel, out_shape=(jax.ShapeDtypeStruct((channels_...  2.45 us
    unnamed x3, local copies, waits for them, and re-layouts  1.65 us
    pallas_call x1, Pallas kernels, spread_records(): pl.pallas_call(spread_kernel, out_shape=jax.ShapeDtypeStruct((count, rows...  1.04 us
  transfers between devices with their start and end apart: 5, of which 3 were waited for; matrix products, arithmetic and copies ran while one was open for 3% of the time, Pallas kernels for 7%

profile of v4, /device:TPU:1, one launch (start us, length us, event | category | flops | bytes accessed | tf_op | source)
XLA Modules:
  0.0 37.6 jit_solution(8836348203091739660)
XLA Ops:
  0.0 0.0 copy-start
  0.0 0.7 %copy-done = f32[19,128]{1,0:T(8,128)S(1)} copy-done((f32[19,128]{1,0:T(8,128)S(1)}, f32[19,128]{1,0:T(8,128)}, u32[]{:S(2)}) %copy-start) | copy-done | bytes 9752
  0.7 1.0 %spread_records.1 = f32[32,24,128]{2,1,0:T(8,128)} custom-call(f32[19,128]{1,0:T(8,128)S(1)} %copy-done), custom_call_target="tpu_custom_call" | custom-call | tf_op jit(solution)/shard_map/spread_records/pallas_call | solution.py:216
  1.8 9.2 %all-to-all-start = ((f32[32,24,128]{2,1,0:T(8,128)}), f32[32,24,128]{2,1,0:T(8,128)S(1)}, u32[]{:S(2)}, u32[]{:S(2)}) async-start(f32[32,24,128]{2,1,0:T(8,128)} %spread_records.1), calls=%async_computation | async-start | bytes 786432 | tf_op jit(solution)/shard_map/all_to_all | solution.py:297
  11.0 0.9 %copy.5.templates_ref = f32[4,19,600]{2,1,0:T(8,128)S(1)} copy(f32[4,19,600]{2,0,1:T(4,128)} %param.5) | data formatting | bytes 364800 | tf_op args[1]
  11.9 2.4 %prepare_weights.1 = (bf16[19,640,128]{2,1,0:T(8,128)(2,1)S(1)}, f32[19,128]{1,0:T(8,128)}) custom-call(f32[4,19,600]{2,1,0:T(8,128)S(1)} %copy.5.templates_ref), custom_call_target="tpu_custom_call" | custom-call | tf_op jit(solution)/shard_map/prepare_weights/pallas_call | solution.py:234
  14.4 5.3 %all-to-all-done = f32[32,24,128]{2,1,0:T(8,128)S(1)} async-done(((f32[32,24,128]{2,1,0:T(8,128)}), f32[32,24,128]{2,1,0:T(8,128)S(1)}, u32[]{:S(2)}, u32[]{:S(2)}) %all-to-all-start) | async-done | bytes 393248 | tf_op jit(solution)/shard_map/all_to_all | solution.py:297
  19.7 2.8 %stack_channels.1.refs_0_ = f32[96,128]{1,0:T(8,128)S(1)} custom-call(s32[4,19]{1,0:T(4,128)} %refs_0_.1, s32[4,19]{1,0:T(4,128)} %refs_1_.1, f32[19,128]{1,0:T(8,128)} %get-tuple-element.7.refs_2_, f32[768,128]{1,0:T(8,128)S(1)} %bitcast.2, bf16[19,640,128]{2,1,0:T(8,128)(2,1)S(1)} %get-tuple-element.8.refs_4_), custom_call_target="tpu_custom_call" | custom-call | tf_op jit(solution)/shard_map/stack_channels/pallas_call | solution.py:254
  22.5 2.6 %collective-permute-start = (f32[96,128]{1,0:T(8,128)S(1)}, f32[96,128]{1,0:T(8,128)S(1)}, u32[]{:S(2)}, u32[]{:S(2)}) collective-permute-start(f32[96,128]{1,0:T(8,128)S(1)} %stack_channels.1.refs_0_), channel_id=1, source_target_pairs={{0,1},{1,0},{2,3},{3,2},{4,5},{5,4},{6,7},{7,6},{8,9},{9,8},{10,11... | collective-permute-start | bytes 147464 | tf_op jit(solution)/shard_map/ppermute | solution.py:288
  25.1 0.9 %collective-permute-done.refs_1_ = f32[96,128]{1,0:T(8,128)S(1)} collective-permute-done((f32[96,128]{1,0:T(8,128)S(1)}, f32[96,128]{1,0:T(8,128)S(1)}, u32[]{:S(2)}, u32[]{:S(2)}) %collective-permute-start) | collective-permute-done | bytes 49184 | tf_op jit(solution)/shard_map/ppermute | solution.py:288
  26.0 6.1 %collective-permute-start.3 = (bf16[96,128]{1,0:T(8,128)(2,1)S(1)}, bf16[96,128]{1,0:T(8,128)(2,1)S(1)}, u32[]{:S(2)}, u32[]{:S(2)}) collective-permute-start(bf16[96,128]{1,0:T(8,128)(2,1)S(1)} %add_convert_fusion), channel_id=1, source_target_pairs={{0,4},{1,5},{2,6},{3,7},{4,0},{5,1},{6,2},{7,3},{8,12},{9,13},{10,... | collective-permute-start | bytes 73736 | tf_op jit(solution)/shard_map/ppermute | solution.py:288
  32.1 0.3 collective-permute-start.2
  32.4 0.9 %collective-permute-start.1 = (bf16[96,128]{1,0:T(8,128)(2,1)S(1)}, bf16[96,128]{1,0:T(8,128)(2,1)S(1)}, u32[]{:S(2)}, u32[]{:S(2)}) collective-permute-start(bf16[96,128]{1,0:T(8,128)(2,1)S(1)} %add_convert_fusion), channel_id=1, source_target_pairs={{0,2},{1,3},{2,0},{3,1},{4,6},{5,7},{6,4},{7,5},{8,10},{9,11},{10,... | collective-permute-start | bytes 73736 | tf_op jit(solution)/shard_map/ppermute | solution.py:288
  33.3 0.0 collective-permute-done.3.refs_4_
  33.3 3.6 %collective-permute-done.2.refs_3_ = bf16[96,128]{1,0:T(8,128)(2,1)S(1)} collective-permute-done((bf16[96,128]{1,0:T(8,128)(2,1)S(1)}, bf16[96,128]{1,0:T(8,128)(2,1)S(1)}, u32[]{:S(2)}, u32[]{:S(2)}) %collective-permute-start.2) | collective-permute-done | bytes 24608 | tf_op jit(solution)/shard_map/ppermute | solution.py:288
  36.9 0.0 collective-permute-done.1.refs_2_
  36.9 0.7 %finish.1 = f32[4,384]{1,0:T(4,128)} custom-call(s32[1]{0:T(128)} %bitcast.place_ref, f32[96,128]{1,0:T(8,128)S(1)} %stack_channels.1.refs_0_, f32[96,128]{1,0:T(8,128)S(1)} %collective-permute-done.refs_1_, bf16[96,128]{1,0:T(8,128)(2,1)S(1)} %collective-permute-done.1.refs_2_, bf16[96,128]{1,0:T(8,128)(2,1)S(1)} %collective-permute-done.2.refs_3_, ...), custom_call_target="tpu_custom_call" | custom-call | tf_op jit(solution)/shard_map/finish/pallas_call | solution.py:276
  (1 shorter events, 0.0 us)
Async XLA Ops:
  0.0 0.7 %copy-start = (f32[19,128]{1,0:T(8,128)S(1)}, f32[19,128]{1,0:T(8,128)}, u32[]{:S(2)}) copy-start(f32[19,128]{1,0:T(8,128)} %records_ref.1) | copy-start | bytes 29188
  1.8 18.0 %all-to-all-start = ((f32[32,24,128]{2,1,0:T(8,128)}), f32[32,24,128]{2,1,0:T(8,128)S(1)}, u32[]{:S(2)}, u32[]{:S(2)}) async-start(f32[32,24,128]{2,1,0:T(8,128)} %spread_records.1), calls=%async_computation | async-start | bytes 786432 | tf_op jit(solution)/shard_map/all_to_all | solution.py:297
  22.5 3.5 %collective-permute-start = (f32[96,128]{1,0:T(8,128)S(1)}, f32[96,128]{1,0:T(8,128)S(1)}, u32[]{:S(2)}, u32[]{:S(2)}) collective-permute-start(f32[96,128]{1,0:T(8,128)S(1)} %stack_channels.1.refs_0_), channel_id=1, source_target_pairs={{0,1},{1,0},{2,3},{3,2},{4,5},{5,4},{6,7},{7,6},{8,9},{9,8},{10,11... | collective-permute-start | bytes 147464 | tf_op jit(solution)/shard_map/ppermute | solution.py:288
  26.0 7.3 %collective-permute-start.3 = (bf16[96,128]{1,0:T(8,128)(2,1)S(1)}, bf16[96,128]{1,0:T(8,128)(2,1)S(1)}, u32[]{:S(2)}, u32[]{:S(2)}) collective-permute-start(bf16[96,128]{1,0:T(8,128)(2,1)S(1)} %add_convert_fusion), channel_id=1, source_target_pairs={{0,4},{1,5},{2,6},{3,7},{4,0},{5,1},{6,2},{7,3},{8,12},{9,13},{10,... | collective-permute-start | bytes 73736 | tf_op jit(solution)/shard_map/ppermute | solution.py:288
  32.1 4.8 %collective-permute-start.2 = (bf16[96,128]{1,0:T(8,128)(2,1)S(1)}, bf16[96,128]{1,0:T(8,128)(2,1)S(1)}, u32[]{:S(2)}, u32[]{:S(2)}) collective-permute-start(bf16[96,128]{1,0:T(8,128)(2,1)S(1)} %add_convert_fusion), channel_id=1, source_target_pairs={{0,6},{1,7},{2,4},{3,5},{4,2},{5,3},{6,0},{7,1},{8,14},{9,15},{10,... | collective-permute-start | bytes 73736 | tf_op jit(solution)/shard_map/ppermute | solution.py:288
  32.4 4.5 %collective-permute-start.1 = (bf16[96,128]{1,0:T(8,128)(2,1)S(1)}, bf16[96,128]{1,0:T(8,128)(2,1)S(1)}, u32[]{:S(2)}, u32[]{:S(2)}) collective-permute-start(bf16[96,128]{1,0:T(8,128)(2,1)S(1)} %add_convert_fusion), channel_id=1, source_target_pairs={{0,2},{1,3},{2,0},{3,1},{4,6},{5,7},{6,4},{7,5},{8,10},{9,11},{10,... | collective-permute-start | bytes 73736 | tf_op jit(solution)/shard_map/ppermute | solution.py:288

commit v5 on v4

--- a/solution.py
+++ b/solution.py
@@ -25,23 +25,21 @@
     return pltpu.CompilerParams(vmem_limit_bytes=mib << 20)
 
 
-def spread_kernel(records_ref, out_ref, tile_ref, sem):
-    tile_ref[...] = jnp.zeros_like(tile_ref)
-    tile_ref[: records_ref.shape[0], :] = records_ref[...]
-    copies = [pltpu.make_async_copy(tile_ref, out_ref.at[i], sem.at[i]) for i in range(out_ref.shape[0])]
-    for copy in copies:
-        copy.start()
-    for copy in copies:
-        copy.wait()
-
-
-def weights_kernel(templates_ref, weights_ref, inv_hbm, inv_ref, lines_ref, chunks_ref, sem):
+def weights_kernel(
+    off_hbm, avail_hbm, templates_ref, weights_ref, inv_ref, coded_ref, off_ref, avail_ref, lines_ref, chunks_ref, sem
+):
     templ_here, channels_here, length = templates_ref.shape
     step = LANES // templ_here
     chunks = weights_ref.shape[1] // step
     groups = lines_ref.shape[0]
     width = templ_here * LANES
     bf16, f32 = jnp.bfloat16, jnp.float32
+    small = [
+        pltpu.make_async_copy(off_hbm, off_ref, sem.at[0]),
+        pltpu.make_async_copy(avail_hbm, avail_ref, sem.at[1]),
+    ]
+    for copy in small:
+        copy.start()
     lines_ref[...] = jnp.zeros_like(lines_ref)
     for t in range(templ_here):
         shapes = templates_ref[t]
@@ -51,8 +49,6 @@
         for q in range(groups):
             here = min(LANES, length - q * LANES)
             lines_ref[q, :channels_here, t * LANES : t * LANES + here] = centred[:, q * LANES : q * LANES + here]
-    inv_out = pltpu.make_async_copy(inv_ref, inv_hbm, sem)
-    inv_out.start()
     col = lax.broadcasted_iota(jnp.int32, (1, width), 1)
     source = LANES * ((col % LANES) // step) + step * (col // LANES) + step - 1 - col % step
     pick = (lax.broadcasted_iota(jnp.int32, (width, width), 0) == source).astype(f32).astype(bf16)
@@ -77,15 +73,17 @@
                 here = following = jnp.zeros((step, LANES), f32)
             weights_ref[c, m * step : (m + 1) * step, :] = jnp.where(inside, here, before).astype(bf16)
             before = following
-    inv_out.wait()
+    for copy in small:
+        copy.wait()
+    coded_ref[...] = 2 * off_ref[...] + avail_ref[...]
 
 
 def stack_kernel(
-    off_hbm, avail_hbm, inv_hbm, records_ref, weights_ref, out_ref,
-    off_ref, avail_ref, inv_ref, pieces_ref, tails_ref, totals_ref, heads_ref, sem, *slots,
+    coded_ref, inv_ref, records_ref, weights_ref, out_ref,
+    picks_ref, pieces_ref, tails_ref, totals_ref, heads_ref, sem, *slots,
     length,
 ):
-    templ_here, channels_here = off_ref.shape
+    templ_here, channels_here = coded_ref.shape
     step = LANES // templ_here
     blocks = tails_ref.shape[1] - SUBLANES
     framed = slots[: len(slots) // 2]
@@ -94,11 +92,8 @@
     lag_blocks = out_ref.shape[0] // templ_here
     taps = weights_ref.shape[1] // LANES
     bf16, f32 = jnp.bfloat16, jnp.float32
-    pairs = [(off_hbm, off_ref), (avail_hbm, avail_ref), (inv_hbm, inv_ref)]
-    small = [pltpu.make_async_copy(*pair, sem.at[i]) for i, pair in enumerate(pairs)]
-    for copy in small:
-        copy.start()
-
+    picks = pltpu.make_async_copy(coded_ref, picks_ref, sem)
+    picks.start()
     row = lax.broadcasted_iota(jnp.int32, (LANES, LANES), 0)
     col = lax.broadcasted_iota(jnp.int32, (LANES, LANES), 1)
     turn = LANES - length % LANES
@@ -114,6 +109,7 @@
                 high = v.astype(bf16)
                 pieces_ref[rows, 0:LANES] = high
                 pieces_ref[rows, LANES : 2 * LANES] = (v - high.astype(f32)).astype(bf16)
+        picks.wait()
         sums = jnp.dot(pieces_ref[...], adder, preferred_element_type=f32)
         count = 2 * channels_here
         for k, ref in enumerate((tails_ref, totals_ref, heads_ref)):
@@ -123,8 +119,6 @@
     stacks = [jnp.zeros((lag_blocks, LANES), f32) for _ in range(templ_here)]
     for ref in framed:
         ref[blocks:, :] = jnp.zeros((SUBLANES, LANES), f32)
-    for copy in small:
-        copy.wait()
 
     whole = length // LANES
     lane = lax.broadcasted_iota(jnp.int32, (blocks, LANES), 1)
@@ -179,15 +173,15 @@
         product = jnp.dot(frames, weights_ref[c], preferred_element_type=f32) * inv_ref[c : c + 1, :]
         correlated = regroup([product[r * blocks : (r + 1) * blocks, :] for r in range(templ_here)], step)
         for t in range(templ_here):
-            start = off_ref[t, c]
-            down = start // LANES
-            over = start % LANES
+            pick = picks_ref[t, c]
+            down = pick // (2 * LANES)
+            over = pick // 2 % LANES
             ref = moved[slot + t]
             ref[:blocks, :] = pltpu.roll(correlated[t] * scale, (LANES - over) % LANES, 1)
             near = ref[pl.ds(down, lag_blocks), :]
             far = ref[pl.ds(down + 1, lag_blocks), :]
             picked = jnp.where(lag_lane < LANES - over, near, far)
-            stacks[t] = stacks[t] + picked * avail_ref[t, c].astype(f32)
+            stacks[t] = stacks[t] + picked * (pick % 2).astype(f32)
 
     for t in range(templ_here):
         out_ref[t * lag_blocks : (t + 1) * lag_blocks, :] = stacks[t]
@@ -212,19 +206,11 @@
 
 
 def spread_records(records, count):
-    rows = padded_rows(records.shape[0])
-    return pl.pallas_call(
-        spread_kernel,
-        out_shape=jax.ShapeDtypeStruct((count, rows, records.shape[1]), records.dtype),
-        in_specs=[VMEM],
-        out_specs=HBM,
-        scratch_shapes=[pltpu.VMEM((rows, records.shape[1]), records.dtype), pltpu.SemaphoreType.DMA((count,))],
-        compiler_params=limit(1),
-        name="spread_records",
-    )(records)
-
-
-def prepared_weights(templates):
+    channels_here, block_len = records.shape
+    return jnp.broadcast_to(records.reshape(1, channels_here, 1, block_len), (count, channels_here, 1, block_len))
+
+
+def prepared_weights(templates, offsets, available):
     templ_here, channels_here, length = templates.shape
     step = LANES // templ_here
     groups = -(-length // LANES)
@@ -235,41 +221,45 @@
         weights_kernel,
         out_shape=(
             jax.ShapeDtypeStruct((channels_here, chunks_of(length, step) * step, LANES), jnp.bfloat16),
-            pltpu.HBM((channels_here, LANES), jnp.float32),
+            jax.ShapeDtypeStruct((channels_here, LANES), jnp.float32),
+            jax.ShapeDtypeStruct(offsets.shape, jnp.int32),
         ),
-        in_specs=[VMEM],
-        out_specs=(VMEM, HBM),
-        scratch_shapes=[pltpu.VMEM((channels_here, LANES), jnp.float32), lines, chunks, pltpu.SemaphoreType.DMA(())],
+        in_specs=[HBM, HBM, VMEM],
+        out_specs=(VMEM, VMEM, VMEM),
+        scratch_shapes=[
+            pltpu.VMEM(offsets.shape, jnp.int32),
+            pltpu.VMEM(offsets.shape, jnp.int32),
+            lines,
+            chunks,
+            pltpu.SemaphoreType.DMA((2,)),
+        ],
         compiler_params=limit(16),
         name="prepare_weights",
-    )(templates)
-
-
-def partial_stacks(blocks, count, weights, inv, offsets, available, lag_count, length):
-    templ_here, channels_here = offsets.shape
-    offsets, available, inv = (pltpu.with_memory_space_constraint(a, pltpu.HBM) for a in (offsets, available, inv))
+    )(*(pltpu.with_memory_space_constraint(a, pltpu.HBM) for a in (offsets, available)), templates)
+
+
+def partial_stacks(blocks, count, weights, inv, coded, lag_count, length):
+    templ_here, channels_here = coded.shape
     lag_blocks = lag_count // LANES
     total_rows = 2 * channels_here * count
     f32 = jnp.float32
     return pl.pallas_call(
         lambda *refs: stack_kernel(*refs, length=length),
         out_shape=jax.ShapeDtypeStruct((templ_here * lag_blocks, LANES), f32),
-        in_specs=[HBM, HBM, HBM, VMEM, VMEM],
+        in_specs=[VMEM, VMEM, VMEM, VMEM],
         out_specs=VMEM,
         scratch_shapes=[
-            pltpu.SMEM(offsets.shape, offsets.dtype),
-            pltpu.SMEM(available.shape, available.dtype),
-            pltpu.VMEM(inv.shape, f32),
+            pltpu.SMEM(coded.shape, coded.dtype),
             pltpu.VMEM((total_rows, 2 * LANES), jnp.bfloat16),
             pltpu.VMEM((2 * channels_here, count + SUBLANES, LANES), f32),
             pltpu.VMEM((2 * channels_here, count + SUBLANES, LANES), f32),
             pltpu.VMEM((2 * channels_here, count + SUBLANES, LANES), f32),
-            pltpu.SemaphoreType.DMA((3,)),
+            pltpu.SemaphoreType.DMA(()),
         ]
         + [pltpu.VMEM((count + SUBLANES, LANES), f32)] * (2 * channels_here * templ_here),
         compiler_params=limit(24),
         name="stack_channels",
-    )(offsets, available, inv, blocks, weights)
+    )(coded, inv, blocks, weights)
 
 
 def finished(place, parts, templ_here, share):
@@ -284,6 +274,9 @@
     )(place, *parts)
 
 
+ORDER = (1, 2, 6)
+
+
 def swapped(array, distance):
     return lax.ppermute(array, "sta", [(i, i ^ distance) for i in range(lax.axis_size("sta"))])
 
@@ -295,12 +288,14 @@
     shares = lax.axis_size("sta")
     lag_count = block_len * count - OFFMAX - length + 1
     blocks = lax.all_to_all(spread_records(records, count), "tmpl", 0, 0, tiled=True)
-    weights, inv = prepared_weights(templates)
-    mine = partial_stacks(blocks.reshape(-1, block_len), count, weights, inv, offsets, available, lag_count, length)
+    weights, inv, coded = prepared_weights(templates, offsets, available)
+    mine = partial_stacks(blocks.reshape(-1, block_len), count, weights, inv, coded, lag_count, length)
     place = lax.axis_index("sta").reshape(1).astype(jnp.int32)
-    theirs = swapped(mine, 1)
-    pair = (mine + theirs).astype(jnp.bfloat16)
-    parts = [mine, theirs] + [swapped(pair, distance) for distance in (2, 6, 4)]
+    bf16, f32 = jnp.bfloat16, jnp.float32
+    parts = [mine]
+    for distance in ORDER:
+        mine = parts[0] if len(parts) == 1 else parts[0] + parts[1].astype(f32)
+        parts = [mine, swapped(mine if distance == 1 else mine.astype(bf16), distance)]
     return finished(place, parts, templ_here, lag_count // shares)
 
 

time: 37.9 us -> 36.2 us (0.955)
  waiting for transfers between devices: 9.81 us -> 8.17 us
  local copies, waits for them, and re-layouts: 1.65 us -> 2.54 us
  Pallas kernels: 6.98 us -> 6.1 us
    broadcast_in_dim x0 -> x1, local copies, waits for them, and re-layouts: none -> 1.59 us  [spread_records(): jnp.broadcast_to(records.reshape(1, channels_here, 1, block_len), (count,...]
    ppermute x4 -> x3, waiting for transfers between devices: 4.47 us -> 3.33 us  [swapped(): lax.ppermute(array, 'sta', [(i, i ^ distance) for i in range(lax.axis_siz...]
    pallas_call x1 -> x0, Pallas kernels: 1.04 us -> none  [spread_records(): pl.pallas_call(spread_kernel, out_shape=jax.ShapeDtypeStruct((count, rows...]
    unnamed x3 -> x1, local copies, waits for them, and re-layouts: 1.65 us -> 0.95 us
    all_to_all x1, waiting for transfers between devices: 5.34 us -> 4.85 us  [shards(): lax.all_to_all(spread_records(records, count), 'tmpl', 0, 0, tiled=True)]
    ppermute x4 -> x3, starting transfers between devices: 9.87 us -> 9.83 us  [swapped(): lax.ppermute(array, 'sta', [(i, i ^ distance) for i in range(lax.axis_siz...]
  transfers between devices with their start and end apart: 5 -> 4, of which waited for: 3 -> 4; matrix products, arithmetic and copies ran while one was open for 3% -> 3% of each run, Pallas kernels for 7% -> 7%
where the time goes in v5:
time: 36.2 us; the launch traced here: 35.9 us
  starting transfers between devices  19 us (52%)
  waiting for transfers between devices  8.17 us (23%)
  Pallas kernels  6.1 us (17%)
  local copies, waits for them, and re-layouts  2.54 us (7%)
    ppermute x3, starting transfers between devices, swapped(): lax.ppermute(array, 'sta', [(i, i ^ distance) for i in range(lax.axis_siz...  9.83 us
    all_to_all x1, starting transfers between devices, shards(): lax.all_to_all(spread_records(records, count), 'tmpl', 0, 0, tiled=True)  9.21 us
    all_to_all x1, waiting for transfers between devices, shards(): lax.all_to_all(spread_records(records, count), 'tmpl', 0, 0, tiled=True)  4.85 us
    ppermute x3, waiting for transfers between devices, swapped(): lax.ppermute(array, 'sta', [(i, i ^ distance) for i in range(lax.axis_siz...  3.33 us
    pallas_call x1, Pallas kernels, partial_stacks(): pl.pallas_call(lambda *refs: stack_kernel(*refs, length=length), out_shap...  2.82 us
    pallas_call x1, Pallas kernels, prepared_weights(): pl.pallas_call(weights_kernel, out_shape=(jax.ShapeDtypeStruct((channels_...  2.57 us
    broadcast_in_dim x1, local copies, waits for them, and re-layouts, spread_records(): jnp.broadcast_to(records.reshape(1, channels_here, 1, block_len), (count,...  1.59 us
    unnamed x1, local copies, waits for them, and re-layouts  0.95 us
  transfers between devices with their start and end apart: 4, of which 4 were waited for; matrix products, arithmetic and copies ran while one was open for 3% of the time, Pallas kernels for 7%

profile of v5, /device:TPU:1, one launch (start us, length us, event | category | flops | bytes accessed | tf_op | source)
XLA Modules:
  0.0 35.9 jit_solution(11944096074072799512)
XLA Ops:
  0.0 1.6 %broadcast_in_dim.2 = f32[32,19,1,128]{3,2,1,0:T(1,128)} broadcast(f32[19,128]{1,0:T(8,128)} %param.4), dimensions={1,3} | broadcast | bytes 321024 | tf_op jit(solution)/shard_map/broadcast_in_dim | solution.py:210
  1.6 9.2 %all-to-all-start = ((f32[32,19,1,128]{3,2,1,0:T(1,128)}), f32[32,19,1,128]{3,2,1,0:T(1,128)S(1)}, u32[]{:S(2)}, u32[]{:S(2)}) async-start(f32[32,19,1,128]{3,2,1,0:T(1,128)} %broadcast_in_dim.2), calls=%async_computation | async-start | bytes 622592 | tf_op jit(solution)/shard_map/all_to_all | solution.py:290
  10.8 0.9 %copy.7.templates_ref = f32[4,19,600]{2,1,0:T(8,128)S(1)} copy(f32[4,19,600]{2,0,1:T(4,128)} %param.5) | data formatting | bytes 364800 | tf_op args[1]
  11.8 2.6 %prepare_weights.1 = (bf16[19,640,128]{2,1,0:T(8,128)(2,1)S(1)}, f32[19,128]{1,0:T(8,128)S(1)}, s32[4,19]{1,0:T(4,128)S(1)}) custom-call(s32[4,19]{1,0:T(4,128)} %off_hbm.1, s32[4,19]{1,0:T(4,128)} %avail_hbm.1, f32[4,19,600]{2,1,0:T(8,128)S(1)} %copy.7.templates_ref), custom_call_target="tpu_custom_call" | custom-call | tf_op jit(solution)/shard_map/prepare_weights/pallas_call | solution.py:220
  14.3 4.8 %all-to-all-done = f32[32,19,1,128]{3,2,1,0:T(1,128)S(1)} async-done(((f32[32,19,1,128]{3,2,1,0:T(1,128)}), f32[32,19,1,128]{3,2,1,0:T(1,128)S(1)}, u32[]{:S(2)}, u32[]{:S(2)}) %all-to-all-start) | async-done | bytes 311328 | tf_op jit(solution)/shard_map/all_to_all | solution.py:290
  19.2 2.8 %stack_channels.1 = f32[96,128]{1,0:T(8,128)S(1)} custom-call(s32[4,19]{1,0:T(4,128)S(1)} %get-tuple-element.8.refs_0_, f32[19,128]{1,0:T(8,128)S(1)} %get-tuple-element.9.refs_1_, f32[608,128]{1,0:T(8,128)S(1)} %bitcast.2, bf16[19,640,128]{2,1,0:T(8,128)(2,1)S(1)} %get-tuple-element.10.refs_3_), custom_call_target="tpu_custom_call" | custom-call | tf_op jit(solution)/shard_map/stack_channels/pallas_call | solution.py:246
  22.0 2.2 %collective-permute-start = (f32[96,128]{1,0:T(8,128)S(1)}, f32[96,128]{1,0:T(8,128)S(1)}, u32[]{:S(2)}, u32[]{:S(2)}) collective-permute-start(f32[96,128]{1,0:T(8,128)S(1)} %stack_channels.1), channel_id=1, source_target_pairs={{0,1},{1,0},{2,3},{3,2},{4,5},{5,4},{6,7},{7,6},{8,9},{9,8},{10,11... | collective-permute-start | bytes 147464 | tf_op jit(solution)/shard_map/ppermute | solution.py:281
  24.2 0.9 %collective-permute-done = f32[96,128]{1,0:T(8,128)S(1)} collective-permute-done((f32[96,128]{1,0:T(8,128)S(1)}, f32[96,128]{1,0:T(8,128)S(1)}, u32[]{:S(2)}, u32[]{:S(2)}) %collective-permute-start) | collective-permute-done | bytes 49184 | tf_op jit(solution)/shard_map/ppermute | solution.py:281
  25.1 3.1 %collective-permute-start.1 = (bf16[96,128]{1,0:T(8,128)(2,1)S(1)}, bf16[96,128]{1,0:T(8,128)(2,1)S(1)}, u32[]{:S(2)}, u32[]{:S(2)}) collective-permute-start(bf16[96,128]{1,0:T(8,128)(2,1)S(1)} %get-tuple-element.13), channel_id=1, source_target_pairs={{0,2},{1,3},{2,0},{3,1},{4,6},{5,7},{6,4},{7,5},{8,10},{9,11},{10,... | collective-permute-start | bytes 73736 | tf_op jit(solution)/shard_map/ppermute | solution.py:281
  28.2 1.2 %collective-permute-done.1 = bf16[96,128]{1,0:T(8,128)(2,1)S(1)} collective-permute-done((bf16[96,128]{1,0:T(8,128)(2,1)S(1)}, bf16[96,128]{1,0:T(8,128)(2,1)S(1)}, u32[]{:S(2)}, u32[]{:S(2)}) %collective-permute-start.1) | collective-permute-done | bytes 24608 | tf_op jit(solution)/shard_map/ppermute | solution.py:281
  29.4 4.6 %collective-permute-start.2 = (bf16[96,128]{1,0:T(8,128)(2,1)S(1)}, bf16[96,128]{1,0:T(8,128)(2,1)S(1)}, u32[]{:S(2)}, u32[]{:S(2)}) collective-permute-start(bf16[96,128]{1,0:T(8,128)(2,1)S(1)} %get-tuple-element.11), channel_id=1, source_target_pairs={{0,6},{1,7},{2,4},{3,5},{4,2},{5,3},{6,0},{7,1},{8,14},{9,15},{10,... | collective-permute-start | bytes 73736 | tf_op jit(solution)/shard_map/ppermute | solution.py:281
  34.0 1.2 %collective-permute-done.2.refs_1_ = bf16[96,128]{1,0:T(8,128)(2,1)S(1)} collective-permute-done((bf16[96,128]{1,0:T(8,128)(2,1)S(1)}, bf16[96,128]{1,0:T(8,128)(2,1)S(1)}, u32[]{:S(2)}, u32[]{:S(2)}) %collective-permute-start.2) | collective-permute-done | bytes 24608 | tf_op jit(solution)/shard_map/ppermute | solution.py:281
  35.2 0.7 %finish.1 = f32[4,384]{1,0:T(4,128)} custom-call(s32[1]{0:T(128)} %bitcast.place_ref, f32[96,128]{1,0:T(8,128)S(1)} %get-tuple-element.12.refs_0_, bf16[96,128]{1,0:T(8,128)(2,1)S(1)} %collective-permute-done.2.refs_1_), custom_call_target="tpu_custom_call" | custom-call | tf_op jit(solution)/shard_map/finish/pallas_call | solution.py:266
  (2 shorter events, 0.0 us)
Async XLA Ops:
  1.6 17.6 %all-to-all-start = ((f32[32,19,1,128]{3,2,1,0:T(1,128)}), f32[32,19,1,128]{3,2,1,0:T(1,128)S(1)}, u32[]{:S(2)}, u32[]{:S(2)}) async-start(f32[32,19,1,128]{3,2,1,0:T(1,128)} %broadcast_in_dim.2), calls=%async_computation | async-start | bytes 622592 | tf_op jit(solution)/shard_map/all_to_all | solution.py:290
  22.0 3.1 %collective-permute-start = (f32[96,128]{1,0:T(8,128)S(1)}, f32[96,128]{1,0:T(8,128)S(1)}, u32[]{:S(2)}, u32[]{:S(2)}) collective-permute-start(f32[96,128]{1,0:T(8,128)S(1)} %stack_channels.1), channel_id=1, source_target_pairs={{0,1},{1,0},{2,3},{3,2},{4,5},{5,4},{6,7},{7,6},{8,9},{9,8},{10,11... | collective-permute-start | bytes 147464 | tf_op jit(solution)/shard_map/ppermute | solution.py:281
  25.1 4.3 %collective-permute-start.1 = (bf16[96,128]{1,0:T(8,128)(2,1)S(1)}, bf16[96,128]{1,0:T(8,128)(2,1)S(1)}, u32[]{:S(2)}, u32[]{:S(2)}) collective-permute-start(bf16[96,128]{1,0:T(8,128)(2,1)S(1)} %get-tuple-element.13), channel_id=1, source_target_pairs={{0,2},{1,3},{2,0},{3,1},{4,6},{5,7},{6,4},{7,5},{8,10},{9,11},{10,... | collective-permute-start | bytes 73736 | tf_op jit(solution)/shard_map/ppermute | solution.py:281
  29.4 5.8 %collective-permute-start.2 = (bf16[96,128]{1,0:T(8,128)(2,1)S(1)}, bf16[96,128]{1,0:T(8,128)(2,1)S(1)}, u32[]{:S(2)}, u32[]{:S(2)}) collective-permute-start(bf16[96,128]{1,0:T(8,128)(2,1)S(1)} %get-tuple-element.11), channel_id=1, source_target_pairs={{0,6},{1,7},{2,4},{3,5},{4,2},{5,3},{6,0},{7,1},{8,14},{9,15},{10,... | collective-permute-start | bytes 73736 | tf_op jit(solution)/shard_map/ppermute | solution.py:281

commit v6 on v5

--- a/solution.py
+++ b/solution.py
@@ -6,7 +6,8 @@
 from jax.sharding import PartitionSpec as P
 
 OFFMAX = 425
-LANES = 128
+LANE_BITS = 7
+LANES = 1 << LANE_BITS
 SUBLANES = 8
 SMEM = pl.BlockSpec(memory_space=pltpu.SMEM)
 VMEM = pl.BlockSpec(memory_space=pltpu.VMEM)
@@ -101,6 +102,8 @@
     adder = jnp.concatenate([kind.astype(f32) for kind in kinds], axis=1).astype(bf16)
     adder = jnp.concatenate([adder, adder], axis=0)
 
+    picks.wait()
+
     def block_sums():
         for c in range(channels_here):
             x = records_ref[pl.ds(c, blocks, stride=pitch), :]
@@ -109,7 +112,6 @@
                 high = v.astype(bf16)
                 pieces_ref[rows, 0:LANES] = high
                 pieces_ref[rows, LANES : 2 * LANES] = (v - high.astype(f32)).astype(bf16)
-        picks.wait()
         sums = jnp.dot(pieces_ref[...], adder, preferred_element_type=f32)
         count = 2 * channels_here
         for k, ref in enumerate((tails_ref, totals_ref, heads_ref)):
@@ -150,12 +152,8 @@
             distance *= 2
         return arrays
 
-    block_sums()
-    for c in range(channels_here):
+    def regrouped(c):
         slot = c * templ_here
-        first = window_sum(2 * c)
-        second = window_sum(2 * c + 1)
-        scale = lax.rsqrt(second - first * first / length + 1e-05)
         here = records_ref[pl.ds(c, blocks, stride=pitch), :]
         framed[slot][:blocks, :] = here
         for r in range(1, templ_here):
@@ -171,17 +169,27 @@
             axis=0,
         )
         product = jnp.dot(frames, weights_ref[c], preferred_element_type=f32) * inv_ref[c : c + 1, :]
-        correlated = regroup([product[r * blocks : (r + 1) * blocks, :] for r in range(templ_here)], step)
+        return regroup([product[r * blocks : (r + 1) * blocks, :] for r in range(templ_here)], step)
+
+    def picked(c, correlated, stacks):
+        slot = c * templ_here
+        first = window_sum(2 * c)
+        second = window_sum(2 * c + 1)
+        scale = lax.rsqrt(second - first * first / length + 1e-05)
         for t in range(templ_here):
             pick = picks_ref[t, c]
-            down = pick // (2 * LANES)
-            over = pick // 2 % LANES
+            down = pick >> LANE_BITS + 1
+            over = (pick >> 1) & (LANES - 1)
             ref = moved[slot + t]
-            ref[:blocks, :] = pltpu.roll(correlated[t] * scale, (LANES - over) % LANES, 1)
+            ref[:blocks, :] = pltpu.roll(correlated[t] * scale, (LANES - over) & (LANES - 1), 1)
             near = ref[pl.ds(down, lag_blocks), :]
             far = ref[pl.ds(down + 1, lag_blocks), :]
-            picked = jnp.where(lag_lane < LANES - over, near, far)
-            stacks[t] = stacks[t] + picked * (pick % 2).astype(f32)
+            lags = jnp.where(lag_lane < LANES - over, near, far)
+            stacks[t] = stacks[t] + lags * (pick & 1).astype(f32)
+
+    block_sums()
+    for c in range(channels_here):
+        picked(c, regrouped(c), stacks)
 
     for t in range(templ_here):
         out_ref[t * lag_blocks : (t + 1) * lag_blocks, :] = stacks[t]

time: 36.2 us -> 35.9 us (level)
  no operation moved by 1% of the time
where the time goes in v6:
time: 35.9 us; the launch traced here: 35.7 us
  starting transfers between devices  19 us (53%)
  waiting for transfers between devices  8.17 us (23%)
  Pallas kernels  5.84 us (16%)
  local copies, waits for them, and re-layouts  2.54 us (7%)
    ppermute x3, starting transfers between devices, swapped(): lax.ppermute(array, 'sta', [(i, i ^ distance) for i in range(lax.axis_siz...  9.83 us
    all_to_all x1, starting transfers between devices, shards(): lax.all_to_all(spread_records(records, count), 'tmpl', 0, 0, tiled=True)  9.21 us
    all_to_all x1, waiting for transfers between devices, shards(): lax.all_to_all(spread_records(records, count), 'tmpl', 0, 0, tiled=True)  4.85 us
    ppermute x3, waiting for transfers between devices, swapped(): lax.ppermute(array, 'sta', [(i, i ^ distance) for i in range(lax.axis_siz...  3.33 us
    pallas_call x1, Pallas kernels, partial_stacks(): pl.pallas_call(lambda *refs: stack_kernel(*refs, length=length), out_shap...  2.57 us
    pallas_call x1, Pallas kernels, prepared_weights(): pl.pallas_call(weights_kernel, out_shape=(jax.ShapeDtypeStruct((channels_...  2.57 us
    broadcast_in_dim x1, local copies, waits for them, and re-layouts, spread_records(): jnp.broadcast_to(records.reshape(1, channels_here, 1, block_len), (count,...  1.59 us
    unnamed x1, local copies, waits for them, and re-layouts  0.95 us
  transfers between devices with their start and end apart: 4, of which 4 were waited for; matrix products, arithmetic and copies ran while one was open for 3% of the time, Pallas kernels for 7%

profile of v6, /device:TPU:1, one launch (start us, length us, event | category | flops | bytes accessed | tf_op | source)
XLA Modules:
  0.0 35.7 jit_solution(1886230460851624228)
XLA Ops:
  0.0 1.6 %broadcast_in_dim.2 = f32[32,19,1,128]{3,2,1,0:T(1,128)} broadcast(f32[19,128]{1,0:T(8,128)} %param.4), dimensions={1,3} | broadcast | bytes 321024 | tf_op jit(solution)/shard_map/broadcast_in_dim | solution.py:218
  1.6 9.2 %all-to-all-start = ((f32[32,19,1,128]{3,2,1,0:T(1,128)}), f32[32,19,1,128]{3,2,1,0:T(1,128)S(1)}, u32[]{:S(2)}, u32[]{:S(2)}) async-start(f32[32,19,1,128]{3,2,1,0:T(1,128)} %broadcast_in_dim.2), calls=%async_computation | async-start | bytes 622592 | tf_op jit(solution)/shard_map/all_to_all | solution.py:298
  10.8 0.9 %copy.7.templates_ref = f32[4,19,600]{2,1,0:T(8,128)S(1)} copy(f32[4,19,600]{2,0,1:T(4,128)} %param.5) | data formatting | bytes 364800 | tf_op args[1]
  11.8 2.6 %prepare_weights.1 = (bf16[19,640,128]{2,1,0:T(8,128)(2,1)S(1)}, f32[19,128]{1,0:T(8,128)S(1)}, s32[4,19]{1,0:T(4,128)S(1)}) custom-call(s32[4,19]{1,0:T(4,128)} %off_hbm.1, s32[4,19]{1,0:T(4,128)} %avail_hbm.1, f32[4,19,600]{2,1,0:T(8,128)S(1)} %copy.7.templates_ref), custom_call_target="tpu_custom_call" | custom-call | tf_op jit(solution)/shard_map/prepare_weights/pallas_call | solution.py:228
  14.3 4.8 %all-to-all-done = f32[32,19,1,128]{3,2,1,0:T(1,128)S(1)} async-done(((f32[32,19,1,128]{3,2,1,0:T(1,128)}), f32[32,19,1,128]{3,2,1,0:T(1,128)S(1)}, u32[]{:S(2)}, u32[]{:S(2)}) %all-to-all-start) | async-done | bytes 311328 | tf_op jit(solution)/shard_map/all_to_all | solution.py:298
  19.2 2.6 %stack_channels.1 = f32[96,128]{1,0:T(8,128)S(1)} custom-call(s32[4,19]{1,0:T(4,128)S(1)} %get-tuple-element.8.refs_0_, f32[19,128]{1,0:T(8,128)S(1)} %get-tuple-element.9.refs_1_, f32[608,128]{1,0:T(8,128)S(1)} %bitcast.2, bf16[19,640,128]{2,1,0:T(8,128)(2,1)S(1)} %get-tuple-element.10.refs_3_), custom_call_target="tpu_custom_call" | custom-call | tf_op jit(solution)/shard_map/stack_channels/pallas_call | solution.py:254
  21.8 2.2 %collective-permute-start = (f32[96,128]{1,0:T(8,128)S(1)}, f32[96,128]{1,0:T(8,128)S(1)}, u32[]{:S(2)}, u32[]{:S(2)}) collective-permute-start(f32[96,128]{1,0:T(8,128)S(1)} %stack_channels.1), channel_id=1, source_target_pairs={{0,1},{1,0},{2,3},{3,2},{4,5},{5,4},{6,7},{7,6},{8,9},{9,8},{10,11... | collective-permute-start | bytes 147464 | tf_op jit(solution)/shard_map/ppermute | solution.py:289
  23.9 0.9 %collective-permute-done = f32[96,128]{1,0:T(8,128)S(1)} collective-permute-done((f32[96,128]{1,0:T(8,128)S(1)}, f32[96,128]{1,0:T(8,128)S(1)}, u32[]{:S(2)}, u32[]{:S(2)}) %collective-permute-start) | collective-permute-done | bytes 49184 | tf_op jit(solution)/shard_map/ppermute | solution.py:289
  24.8 3.1 %collective-permute-start.1 = (bf16[96,128]{1,0:T(8,128)(2,1)S(1)}, bf16[96,128]{1,0:T(8,128)(2,1)S(1)}, u32[]{:S(2)}, u32[]{:S(2)}) collective-permute-start(bf16[96,128]{1,0:T(8,128)(2,1)S(1)} %get-tuple-element.13), channel_id=1, source_target_pairs={{0,2},{1,3},{2,0},{3,1},{4,6},{5,7},{6,4},{7,5},{8,10},{9,11},{10,... | collective-permute-start | bytes 73736 | tf_op jit(solution)/shard_map/ppermute | solution.py:289
  27.9 1.2 %collective-permute-done.1 = bf16[96,128]{1,0:T(8,128)(2,1)S(1)} collective-permute-done((bf16[96,128]{1,0:T(8,128)(2,1)S(1)}, bf16[96,128]{1,0:T(8,128)(2,1)S(1)}, u32[]{:S(2)}, u32[]{:S(2)}) %collective-permute-start.1) | collective-permute-done | bytes 24608 | tf_op jit(solution)/shard_map/ppermute | solution.py:289
  29.2 4.6 %collective-permute-start.2 = (bf16[96,128]{1,0:T(8,128)(2,1)S(1)}, bf16[96,128]{1,0:T(8,128)(2,1)S(1)}, u32[]{:S(2)}, u32[]{:S(2)}) collective-permute-start(bf16[96,128]{1,0:T(8,128)(2,1)S(1)} %get-tuple-element.11), channel_id=1, source_target_pairs={{0,6},{1,7},{2,4},{3,5},{4,2},{5,3},{6,0},{7,1},{8,14},{9,15},{10,... | collective-permute-start | bytes 73736 | tf_op jit(solution)/shard_map/ppermute | solution.py:289
  33.7 1.2 %collective-permute-done.2.refs_1_ = bf16[96,128]{1,0:T(8,128)(2,1)S(1)} collective-permute-done((bf16[96,128]{1,0:T(8,128)(2,1)S(1)}, bf16[96,128]{1,0:T(8,128)(2,1)S(1)}, u32[]{:S(2)}, u32[]{:S(2)}) %collective-permute-start.2) | collective-permute-done | bytes 24608 | tf_op jit(solution)/shard_map/ppermute | solution.py:289
  34.9 0.7 %finish.1 = f32[4,384]{1,0:T(4,128)} custom-call(s32[1]{0:T(128)} %bitcast.place_ref, f32[96,128]{1,0:T(8,128)S(1)} %get-tuple-element.12.refs_0_, bf16[96,128]{1,0:T(8,128)(2,1)S(1)} %collective-permute-done.2.refs_1_), custom_call_target="tpu_custom_call" | custom-call | tf_op jit(solution)/shard_map/finish/pallas_call | solution.py:274
  (2 shorter events, 0.0 us)
Async XLA Ops:
  1.6 17.6 %all-to-all-start = ((f32[32,19,1,128]{3,2,1,0:T(1,128)}), f32[32,19,1,128]{3,2,1,0:T(1,128)S(1)}, u32[]{:S(2)}, u32[]{:S(2)}) async-start(f32[32,19,1,128]{3,2,1,0:T(1,128)} %broadcast_in_dim.2), calls=%async_computation | async-start | bytes 622592 | tf_op jit(solution)/shard_map/all_to_all | solution.py:298
  21.8 3.1 %collective-permute-start = (f32[96,128]{1,0:T(8,128)S(1)}, f32[96,128]{1,0:T(8,128)S(1)}, u32[]{:S(2)}, u32[]{:S(2)}) collective-permute-start(f32[96,128]{1,0:T(8,128)S(1)} %stack_channels.1), channel_id=1, source_target_pairs={{0,1},{1,0},{2,3},{3,2},{4,5},{5,4},{6,7},{7,6},{8,9},{9,8},{10,11... | collective-permute-start | bytes 147464 | tf_op jit(solution)/shard_map/ppermute | solution.py:289
  24.8 4.3 %collective-permute-start.1 = (bf16[96,128]{1,0:T(8,128)(2,1)S(1)}, bf16[96,128]{1,0:T(8,128)(2,1)S(1)}, u32[]{:S(2)}, u32[]{:S(2)}) collective-permute-start(bf16[96,128]{1,0:T(8,128)(2,1)S(1)} %get-tuple-element.13), channel_id=1, source_target_pairs={{0,2},{1,3},{2,0},{3,1},{4,6},{5,7},{6,4},{7,5},{8,10},{9,11},{10,... | collective-permute-start | bytes 73736 | tf_op jit(solution)/shard_map/ppermute | solution.py:289
  29.2 5.8 %collective-permute-start.2 = (bf16[96,128]{1,0:T(8,128)(2,1)S(1)}, bf16[96,128]{1,0:T(8,128)(2,1)S(1)}, u32[]{:S(2)}, u32[]{:S(2)}) collective-permute-start(bf16[96,128]{1,0:T(8,128)(2,1)S(1)} %get-tuple-element.11), channel_id=1, source_target_pairs={{0,6},{1,7},{2,4},{3,5},{4,2},{5,3},{6,0},{7,1},{8,14},{9,15},{10,... | collective-permute-start | bytes 73736 | tf_op jit(solution)/shard_map/ppermute | solution.py:289

commit v7 on v6

--- a/solution.py
+++ b/solution.py
@@ -136,21 +136,17 @@
         ends = jnp.where(lane < turn, at(heads_ref, whole), at(totals_ref, whole) + at(heads_ref, whole + 1))
         return total + ends
 
-    def regroup(arrays, group):
+    def diagonals(arrays):
         count = len(arrays)
-        distance = 1
-        while distance < count:
-            kept = (lane // group) // distance % 2 == 0
-            swapped = list(arrays)
-            for r in range(count):
-                if r // distance % 2 == 0:
-                    a, b = arrays[r], arrays[r + distance]
-                    shift = group * distance
-                    swapped[r] = jnp.where(kept, a, pltpu.roll(b, shift, 1))
-                    swapped[r + distance] = jnp.where(kept, pltpu.roll(a, LANES - shift, 1), b)
-            arrays = swapped
-            distance *= 2
-        return arrays
+        moved_on = [arrays[0]] + [pltpu.roll(arrays[r], r * step, 1) for r in range(1, count)]
+        block = lane // step
+        out = []
+        for t in range(count):
+            line = moved_on[0]
+            for r in range(1, count):
+                line = jnp.where(block == (t + r) % count, moved_on[r], line)
+            out.append(line)
+        return out
 
     def regrouped(c):
         slot = c * templ_here
@@ -169,7 +165,7 @@
             axis=0,
         )
         product = jnp.dot(frames, weights_ref[c], preferred_element_type=f32) * inv_ref[c : c + 1, :]
-        return regroup([product[r * blocks : (r + 1) * blocks, :] for r in range(templ_here)], step)
+        return diagonals([product[r * blocks : (r + 1) * blocks, :] for r in range(templ_here)])
 
     def picked(c, correlated, stacks):
         slot = c * templ_here
@@ -181,7 +177,8 @@
             down = pick >> LANE_BITS + 1
             over = (pick >> 1) & (LANES - 1)
             ref = moved[slot + t]
-            ref[:blocks, :] = pltpu.roll(correlated[t] * scale, (LANES - over) & (LANES - 1), 1)
+            turned = pltpu.roll(scale, t * step, 1) if t else scale
+            ref[:blocks, :] = pltpu.roll(correlated[t] * turned, (2 * LANES - t * step - over) & (LANES - 1), 1)
             near = ref[pl.ds(down, lag_blocks), :]
             far = ref[pl.ds(down + 1, lag_blocks), :]
             lags = jnp.where(lag_lane < LANES - over, near, far)

time: 35.9 us -> 35.8 us (level)
  no operation moved by 1% of the time
where the time goes in v7:
time: 35.8 us; the launch traced here: 35.5 us
  starting transfers between devices  19 us (53%)
  waiting for transfers between devices  8.17 us (23%)
  Pallas kernels  5.73 us (16%)
  local copies, waits for them, and re-layouts  2.54 us (7%)
    ppermute x3, starting transfers between devices, swapped(): lax.ppermute(array, 'sta', [(i, i ^ distance) for i in range(lax.axis_siz...  9.83 us
    all_to_all x1, starting transfers between devices, shards(): lax.all_to_all(spread_records(records, count), 'tmpl', 0, 0, tiled=True)  9.21 us
    all_to_all x1, waiting for transfers between devices, shards(): lax.all_to_all(spread_records(records, count), 'tmpl', 0, 0, tiled=True)  4.85 us
    ppermute x3, waiting for transfers between devices, swapped(): lax.ppermute(array, 'sta', [(i, i ^ distance) for i in range(lax.axis_siz...  3.33 us
    pallas_call x1, Pallas kernels, prepared_weights(): pl.pallas_call(weights_kernel, out_shape=(jax.ShapeDtypeStruct((channels_...  2.57 us
    pallas_call x1, Pallas kernels, partial_stacks(): pl.pallas_call(lambda *refs: stack_kernel(*refs, length=length), out_shap...  2.46 us
    broadcast_in_dim x1, local copies, waits for them, and re-layouts, spread_records(): jnp.broadcast_to(records.reshape(1, channels_here, 1, block_len), (count,...  1.59 us
    unnamed x1, local copies, waits for them, and re-layouts  0.95 us
  transfers between devices with their start and end apart: 4, of which 4 were waited for; matrix products, arithmetic and copies ran while one was open for 3% of the time, Pallas kernels for 7%

profile of v7, /device:TPU:1, one launch (start us, length us, event | category | flops | bytes accessed | tf_op | source)
XLA Modules:
  0.0 35.5 jit_solution(25050989543597492)
XLA Ops:
  0.0 1.6 %broadcast_in_dim.2 = f32[32,19,1,128]{3,2,1,0:T(1,128)} broadcast(f32[19,128]{1,0:T(8,128)} %param.4), dimensions={1,3} | broadcast | bytes 321024 | tf_op jit(solution)/shard_map/broadcast_in_dim | solution.py:215
  1.6 9.2 %all-to-all-start = ((f32[32,19,1,128]{3,2,1,0:T(1,128)}), f32[32,19,1,128]{3,2,1,0:T(1,128)S(1)}, u32[]{:S(2)}, u32[]{:S(2)}) async-start(f32[32,19,1,128]{3,2,1,0:T(1,128)} %broadcast_in_dim.2), calls=%async_computation | async-start | bytes 622592 | tf_op jit(solution)/shard_map/all_to_all | solution.py:295
  10.8 0.9 %copy.7.templates_ref = f32[4,19,600]{2,1,0:T(8,128)S(1)} copy(f32[4,19,600]{2,0,1:T(4,128)} %param.5) | data formatting | bytes 364800 | tf_op args[1]
  11.8 2.6 %prepare_weights.1 = (bf16[19,640,128]{2,1,0:T(8,128)(2,1)S(1)}, f32[19,128]{1,0:T(8,128)S(1)}, s32[4,19]{1,0:T(4,128)S(1)}) custom-call(s32[4,19]{1,0:T(4,128)} %off_hbm.1, s32[4,19]{1,0:T(4,128)} %avail_hbm.1, f32[4,19,600]{2,1,0:T(8,128)S(1)} %copy.7.templates_ref), custom_call_target="tpu_custom_call" | custom-call | tf_op jit(solution)/shard_map/prepare_weights/pallas_call | solution.py:225
  14.3 4.8 %all-to-all-done = f32[32,19,1,128]{3,2,1,0:T(1,128)S(1)} async-done(((f32[32,19,1,128]{3,2,1,0:T(1,128)}), f32[32,19,1,128]{3,2,1,0:T(1,128)S(1)}, u32[]{:S(2)}, u32[]{:S(2)}) %all-to-all-start) | async-done | bytes 311328 | tf_op jit(solution)/shard_map/all_to_all | solution.py:295
  19.2 2.5 %stack_channels.1 = f32[96,128]{1,0:T(8,128)S(1)} custom-call(s32[4,19]{1,0:T(4,128)S(1)} %get-tuple-element.8.refs_0_, f32[19,128]{1,0:T(8,128)S(1)} %get-tuple-element.9.refs_1_, f32[608,128]{1,0:T(8,128)S(1)} %bitcast.2, bf16[19,640,128]{2,1,0:T(8,128)(2,1)S(1)} %get-tuple-element.10.refs_3_), custom_call_target="tpu_custom_call" | custom-call | tf_op jit(solution)/shard_map/stack_channels/pallas_call | solution.py:251
  21.6 2.2 %collective-permute-start = (f32[96,128]{1,0:T(8,128)S(1)}, f32[96,128]{1,0:T(8,128)S(1)}, u32[]{:S(2)}, u32[]{:S(2)}) collective-permute-start(f32[96,128]{1,0:T(8,128)S(1)} %stack_channels.1), channel_id=1, source_target_pairs={{0,1},{1,0},{2,3},{3,2},{4,5},{5,4},{6,7},{7,6},{8,9},{9,8},{10,11... | collective-permute-start | bytes 147464 | tf_op jit(solution)/shard_map/ppermute | solution.py:286
  23.8 0.9 %collective-permute-done = f32[96,128]{1,0:T(8,128)S(1)} collective-permute-done((f32[96,128]{1,0:T(8,128)S(1)}, f32[96,128]{1,0:T(8,128)S(1)}, u32[]{:S(2)}, u32[]{:S(2)}) %collective-permute-start) | collective-permute-done | bytes 49184 | tf_op jit(solution)/shard_map/ppermute | solution.py:286
  24.7 3.1 %collective-permute-start.1 = (bf16[96,128]{1,0:T(8,128)(2,1)S(1)}, bf16[96,128]{1,0:T(8,128)(2,1)S(1)}, u32[]{:S(2)}, u32[]{:S(2)}) collective-permute-start(bf16[96,128]{1,0:T(8,128)(2,1)S(1)} %get-tuple-element.13), channel_id=1, source_target_pairs={{0,2},{1,3},{2,0},{3,1},{4,6},{5,7},{6,4},{7,5},{8,10},{9,11},{10,... | collective-permute-start | bytes 73736 | tf_op jit(solution)/shard_map/ppermute | solution.py:286
  27.8 1.2 %collective-permute-done.1 = bf16[96,128]{1,0:T(8,128)(2,1)S(1)} collective-permute-done((bf16[96,128]{1,0:T(8,128)(2,1)S(1)}, bf16[96,128]{1,0:T(8,128)(2,1)S(1)}, u32[]{:S(2)}, u32[]{:S(2)}) %collective-permute-start.1) | collective-permute-done | bytes 24608 | tf_op jit(solution)/shard_map/ppermute | solution.py:286
  29.0 4.6 %collective-permute-start.2 = (bf16[96,128]{1,0:T(8,128)(2,1)S(1)}, bf16[96,128]{1,0:T(8,128)(2,1)S(1)}, u32[]{:S(2)}, u32[]{:S(2)}) collective-permute-start(bf16[96,128]{1,0:T(8,128)(2,1)S(1)} %get-tuple-element.11), channel_id=1, source_target_pairs={{0,6},{1,7},{2,4},{3,5},{4,2},{5,3},{6,0},{7,1},{8,14},{9,15},{10,... | collective-permute-start | bytes 73736 | tf_op jit(solution)/shard_map/ppermute | solution.py:286
  33.6 1.2 %collective-permute-done.2.refs_1_ = bf16[96,128]{1,0:T(8,128)(2,1)S(1)} collective-permute-done((bf16[96,128]{1,0:T(8,128)(2,1)S(1)}, bf16[96,128]{1,0:T(8,128)(2,1)S(1)}, u32[]{:S(2)}, u32[]{:S(2)}) %collective-permute-start.2) | collective-permute-done | bytes 24608 | tf_op jit(solution)/shard_map/ppermute | solution.py:286
  34.8 0.7 %finish.1 = f32[4,384]{1,0:T(4,128)} custom-call(s32[1]{0:T(128)} %bitcast.place_ref, f32[96,128]{1,0:T(8,128)S(1)} %get-tuple-element.12.refs_0_, bf16[96,128]{1,0:T(8,128)(2,1)S(1)} %collective-permute-done.2.refs_1_), custom_call_target="tpu_custom_call" | custom-call | tf_op jit(solution)/shard_map/finish/pallas_call | solution.py:271
  (2 shorter events, 0.0 us)
Async XLA Ops:
  1.6 17.6 %all-to-all-start = ((f32[32,19,1,128]{3,2,1,0:T(1,128)}), f32[32,19,1,128]{3,2,1,0:T(1,128)S(1)}, u32[]{:S(2)}, u32[]{:S(2)}) async-start(f32[32,19,1,128]{3,2,1,0:T(1,128)} %broadcast_in_dim.2), calls=%async_computation | async-start | bytes 622592 | tf_op jit(solution)/shard_map/all_to_all | solution.py:295
  21.6 3.1 %collective-permute-start = (f32[96,128]{1,0:T(8,128)S(1)}, f32[96,128]{1,0:T(8,128)S(1)}, u32[]{:S(2)}, u32[]{:S(2)}) collective-permute-start(f32[96,128]{1,0:T(8,128)S(1)} %stack_channels.1), channel_id=1, source_target_pairs={{0,1},{1,0},{2,3},{3,2},{4,5},{5,4},{6,7},{7,6},{8,9},{9,8},{10,11... | collective-permute-start | bytes 147464 | tf_op jit(solution)/shard_map/ppermute | solution.py:286
  24.7 4.3 %collective-permute-start.1 = (bf16[96,128]{1,0:T(8,128)(2,1)S(1)}, bf16[96,128]{1,0:T(8,128)(2,1)S(1)}, u32[]{:S(2)}, u32[]{:S(2)}) collective-permute-start(bf16[96,128]{1,0:T(8,128)(2,1)S(1)} %get-tuple-element.13), channel_id=1, source_target_pairs={{0,2},{1,3},{2,0},{3,1},{4,6},{5,7},{6,4},{7,5},{8,10},{9,11},{10,... | collective-permute-start | bytes 73736 | tf_op jit(solution)/shard_map/ppermute | solution.py:286
  29.0 5.8 %collective-permute-start.2 = (bf16[96,128]{1,0:T(8,128)(2,1)S(1)}, bf16[96,128]{1,0:T(8,128)(2,1)S(1)}, u32[]{:S(2)}, u32[]{:S(2)}) collective-permute-start(bf16[96,128]{1,0:T(8,128)(2,1)S(1)} %get-tuple-element.11), channel_id=1, source_target_pairs={{0,6},{1,7},{2,4},{3,5},{4,2},{5,3},{6,0},{7,1},{8,14},{9,15},{10,... | collective-permute-start | bytes 73736 | tf_op jit(solution)/shard_map/ppermute | solution.py:286

commit v8 on v7

--- a/solution.py
+++ b/solution.py
@@ -210,9 +210,24 @@
             out_ref[t : t + 1, i * LANES : (i + 1) * LANES] = line * unit
 
 
+def spread_kernel(records_ref, out_ref):
+    channels_here = records_ref.shape[0]
+    block = records_ref[...]
+    for i in range(out_ref.shape[0] // channels_here):
+        out_ref[i * channels_here : (i + 1) * channels_here, :] = block
+
+
 def spread_records(records, count):
     channels_here, block_len = records.shape
-    return jnp.broadcast_to(records.reshape(1, channels_here, 1, block_len), (count, channels_here, 1, block_len))
+    copies = pl.pallas_call(
+        spread_kernel,
+        out_shape=jax.ShapeDtypeStruct((count * channels_here, block_len), records.dtype),
+        in_specs=[VMEM],
+        out_specs=VMEM,
+        compiler_params=limit(2),
+        name="spread_records",
+    )(records)
+    return copies.reshape(count, channels_here, 1, block_len)
 
 
 def prepared_weights(templates, offsets, available):

time: 35.8 us -> 35.7 us (level)
  local copies, waits for them, and re-layouts: 2.54 us -> 1.65 us
  Pallas kernels: 5.73 us -> 6.47 us
    broadcast_in_dim x1 -> x0, local copies, waits for them, and re-layouts: 1.59 us -> none  [spread_records(): jnp.broadcast_to(records.reshape(1, channels_here, 1, block_len), (count,...]
    pallas_call x0 -> x1, Pallas kernels: none -> 0.75 us  [spread_records(): pl.pallas_call(spread_kernel, out_shape=jax.ShapeDtypeStruct((count * cha...]
    unnamed x1 -> x3, local copies, waits for them, and re-layouts: 0.95 us -> 1.65 us
where the time goes in v8:
time: 35.7 us; the launch traced here: 35.4 us
  starting transfers between devices  19 us (53%)
  waiting for transfers between devices  8.17 us (23%)
  Pallas kernels  6.47 us (18%)
  local copies, waits for them, and re-layouts  1.65 us (5%)
    ppermute x3, starting transfers between devices, swapped(): lax.ppermute(array, 'sta', [(i, i ^ distance) for i in range(lax.axis_siz...  9.83 us
    all_to_all x1, starting transfers between devices, shards(): lax.all_to_all(spread_records(records, count), 'tmpl', 0, 0, tiled=True)  9.21 us
    all_to_all x1, waiting for transfers between devices, shards(): lax.all_to_all(spread_records(records, count), 'tmpl', 0, 0, tiled=True)  4.85 us
    ppermute x3, waiting for transfers between devices, swapped(): lax.ppermute(array, 'sta', [(i, i ^ distance) for i in range(lax.axis_siz...  3.33 us
    pallas_call x1, Pallas kernels, prepared_weights(): pl.pallas_call(weights_kernel, out_shape=(jax.ShapeDtypeStruct((channels_...  2.57 us
    pallas_call x1, Pallas kernels, partial_stacks(): pl.pallas_call(lambda *refs: stack_kernel(*refs, length=length), out_shap...  2.45 us
    unnamed x3, local copies, waits for them, and re-layouts  1.65 us
    pallas_call x1, Pallas kernels, spread_records(): pl.pallas_call(spread_kernel, out_shape=jax.ShapeDtypeStruct((count * cha...  0.75 us
  transfers between devices with their start and end apart: 4, of which 4 were waited for; matrix products, arithmetic and copies ran while one was open for 3% of the time, Pallas kernels for 7%

profile of v8, /device:TPU:1, one launch (start us, length us, event | category | flops | bytes accessed | tf_op | source)
XLA Modules:
  0.0 35.4 jit_solution(14785426648083040670)
XLA Ops:
  0.0 0.0 copy-start
  0.0 0.7 %copy-done = f32[19,128]{1,0:T(8,128)S(1)} copy-done((f32[19,128]{1,0:T(8,128)S(1)}, f32[19,128]{1,0:T(8,128)}, u32[]{:S(2)}) %copy-start) | copy-done | bytes 9752
  0.7 0.7 %spread_records.1 = f32[608,128]{1,0:T(8,128)} custom-call(f32[19,128]{1,0:T(8,128)S(1)} %copy-done), custom_call_target="tpu_custom_call" | custom-call | tf_op jit(solution)/shard_map/spread_records/pallas_call | solution.py:222
  1.5 9.2 %all-to-all-start = ((f32[32,19,1,128]{3,2,1,0:T(1,128)}), f32[32,19,1,128]{3,2,1,0:T(1,128)S(1)}, u32[]{:S(2)}, u32[]{:S(2)}) async-start(f32[32,19,1,128]{3,2,1,0:T(1,128)} %bitcast.1), calls=%async_computation | async-start | bytes 622592 | tf_op jit(solution)/shard_map/all_to_all | solution.py:310
  10.7 0.9 %copy.7.templates_ref = f32[4,19,600]{2,1,0:T(8,128)S(1)} copy(f32[4,19,600]{2,0,1:T(4,128)} %param.5) | data formatting | bytes 364800 | tf_op args[1]
  11.6 2.6 %prepare_weights.1 = (bf16[19,640,128]{2,1,0:T(8,128)(2,1)S(1)}, f32[19,128]{1,0:T(8,128)S(1)}, s32[4,19]{1,0:T(4,128)S(1)}) custom-call(s32[4,19]{1,0:T(4,128)} %off_hbm.1, s32[4,19]{1,0:T(4,128)} %avail_hbm.1, f32[4,19,600]{2,1,0:T(8,128)S(1)} %copy.7.templates_ref), custom_call_target="tpu_custom_call" | custom-call | tf_op jit(solution)/shard_map/prepare_weights/pallas_call | solution.py:240
  14.2 4.8 %all-to-all-done = f32[32,19,1,128]{3,2,1,0:T(1,128)S(1)} async-done(((f32[32,19,1,128]{3,2,1,0:T(1,128)}), f32[32,19,1,128]{3,2,1,0:T(1,128)S(1)}, u32[]{:S(2)}, u32[]{:S(2)}) %all-to-all-start) | async-done | bytes 311328 | tf_op jit(solution)/shard_map/all_to_all | solution.py:310
  19.0 2.4 %stack_channels.1 = f32[96,128]{1,0:T(8,128)S(1)} custom-call(s32[4,19]{1,0:T(4,128)S(1)} %get-tuple-element.8.refs_0_, f32[19,128]{1,0:T(8,128)S(1)} %get-tuple-element.9.refs_1_, f32[608,128]{1,0:T(8,128)S(1)} %bitcast.3, bf16[19,640,128]{2,1,0:T(8,128)(2,1)S(1)} %get-tuple-element.10.refs_3_), custom_call_target="tpu_custom_call" | custom-call | tf_op jit(solution)/shard_map/stack_channels/pallas_call | solution.py:266
  21.5 2.2 %collective-permute-start = (f32[96,128]{1,0:T(8,128)S(1)}, f32[96,128]{1,0:T(8,128)S(1)}, u32[]{:S(2)}, u32[]{:S(2)}) collective-permute-start(f32[96,128]{1,0:T(8,128)S(1)} %stack_channels.1), channel_id=1, source_target_pairs={{0,1},{1,0},{2,3},{3,2},{4,5},{5,4},{6,7},{7,6},{8,9},{9,8},{10,11... | collective-permute-start | bytes 147464 | tf_op jit(solution)/shard_map/ppermute | solution.py:301
  23.7 0.9 %collective-permute-done = f32[96,128]{1,0:T(8,128)S(1)} collective-permute-done((f32[96,128]{1,0:T(8,128)S(1)}, f32[96,128]{1,0:T(8,128)S(1)}, u32[]{:S(2)}, u32[]{:S(2)}) %collective-permute-start) | collective-permute-done | bytes 49184 | tf_op jit(solution)/shard_map/ppermute | solution.py:301
  24.6 3.1 %collective-permute-start.1 = (bf16[96,128]{1,0:T(8,128)(2,1)S(1)}, bf16[96,128]{1,0:T(8,128)(2,1)S(1)}, u32[]{:S(2)}, u32[]{:S(2)}) collective-permute-start(bf16[96,128]{1,0:T(8,128)(2,1)S(1)} %get-tuple-element.13), channel_id=1, source_target_pairs={{0,2},{1,3},{2,0},{3,1},{4,6},{5,7},{6,4},{7,5},{8,10},{9,11},{10,... | collective-permute-start | bytes 73736 | tf_op jit(solution)/shard_map/ppermute | solution.py:301
  27.7 1.2 %collective-permute-done.1 = bf16[96,128]{1,0:T(8,128)(2,1)S(1)} collective-permute-done((bf16[96,128]{1,0:T(8,128)(2,1)S(1)}, bf16[96,128]{1,0:T(8,128)(2,1)S(1)}, u32[]{:S(2)}, u32[]{:S(2)}) %collective-permute-start.1) | collective-permute-done | bytes 24608 | tf_op jit(solution)/shard_map/ppermute | solution.py:301
  28.9 4.6 %collective-permute-start.2 = (bf16[96,128]{1,0:T(8,128)(2,1)S(1)}, bf16[96,128]{1,0:T(8,128)(2,1)S(1)}, u32[]{:S(2)}, u32[]{:S(2)}) collective-permute-start(bf16[96,128]{1,0:T(8,128)(2,1)S(1)} %get-tuple-element.11), channel_id=1, source_target_pairs={{0,6},{1,7},{2,4},{3,5},{4,2},{5,3},{6,0},{7,1},{8,14},{9,15},{10,... | collective-permute-start | bytes 73736 | tf_op jit(solution)/shard_map/ppermute | solution.py:301
  33.5 1.2 %collective-permute-done.2.refs_1_ = bf16[96,128]{1,0:T(8,128)(2,1)S(1)} collective-permute-done((bf16[96,128]{1,0:T(8,128)(2,1)S(1)}, bf16[96,128]{1,0:T(8,128)(2,1)S(1)}, u32[]{:S(2)}, u32[]{:S(2)}) %collective-permute-start.2) | collective-permute-done | bytes 24608 | tf_op jit(solution)/shard_map/ppermute | solution.py:301
  34.7 0.7 %finish.1 = f32[4,384]{1,0:T(4,128)} custom-call(s32[1]{0:T(128)} %bitcast.place_ref, f32[96,128]{1,0:T(8,128)S(1)} %get-tuple-element.12.refs_0_, bf16[96,128]{1,0:T(8,128)(2,1)S(1)} %collective-permute-done.2.refs_1_), custom_call_target="tpu_custom_call" | custom-call | tf_op jit(solution)/shard_map/finish/pallas_call | solution.py:286
  (2 shorter events, 0.0 us)
Async XLA Ops:
  0.0 0.7 %copy-start = (f32[19,128]{1,0:T(8,128)S(1)}, f32[19,128]{1,0:T(8,128)}, u32[]{:S(2)}) copy-start(f32[19,128]{1,0:T(8,128)} %records_ref.1) | copy-start | bytes 29188
  1.5 17.6 %all-to-all-start = ((f32[32,19,1,128]{3,2,1,0:T(1,128)}), f32[32,19,1,128]{3,2,1,0:T(1,128)S(1)}, u32[]{:S(2)}, u32[]{:S(2)}) async-start(f32[32,19,1,128]{3,2,1,0:T(1,128)} %bitcast.1), calls=%async_computation | async-start | bytes 622592 | tf_op jit(solution)/shard_map/all_to_all | solution.py:310
  21.5 3.1 %collective-permute-start = (f32[96,128]{1,0:T(8,128)S(1)}, f32[96,128]{1,0:T(8,128)S(1)}, u32[]{:S(2)}, u32[]{:S(2)}) collective-permute-start(f32[96,128]{1,0:T(8,128)S(1)} %stack_channels.1), channel_id=1, source_target_pairs={{0,1},{1,0},{2,3},{3,2},{4,5},{5,4},{6,7},{7,6},{8,9},{9,8},{10,11... | collective-permute-start | bytes 147464 | tf_op jit(solution)/shard_map/ppermute | solution.py:301
  24.6 4.3 %collective-permute-start.1 = (bf16[96,128]{1,0:T(8,128)(2,1)S(1)}, bf16[96,128]{1,0:T(8,128)(2,1)S(1)}, u32[]{:S(2)}, u32[]{:S(2)}) collective-permute-start(bf16[96,128]{1,0:T(8,128)(2,1)S(1)} %get-tuple-element.13), channel_id=1, source_target_pairs={{0,2},{1,3},{2,0},{3,1},{4,6},{5,7},{6,4},{7,5},{8,10},{9,11},{10,... | collective-permute-start | bytes 73736 | tf_op jit(solution)/shard_map/ppermute | solution.py:301
  28.9 5.8 %collective-permute-start.2 = (bf16[96,128]{1,0:T(8,128)(2,1)S(1)}, bf16[96,128]{1,0:T(8,128)(2,1)S(1)}, u32[]{:S(2)}, u32[]{:S(2)}) collective-permute-start(bf16[96,128]{1,0:T(8,128)(2,1)S(1)} %get-tuple-element.11), channel_id=1, source_target_pairs={{0,6},{1,7},{2,4},{3,5},{4,2},{5,3},{6,0},{7,1},{8,14},{9,15},{10,... | collective-permute-start | bytes 73736 | tf_op jit(solution)/shard_map/ppermute | solution.py:301

commit v9 on v8

--- a/solution.py
+++ b/solution.py
@@ -86,7 +86,7 @@
 ):
     templ_here, channels_here = coded_ref.shape
     step = LANES // templ_here
-    blocks = tails_ref.shape[1] - SUBLANES
+    blocks = tails_ref.shape[1]
     framed = slots[: len(slots) // 2]
     moved = slots[len(slots) // 2 :]
     pitch = records_ref.shape[0] // blocks
@@ -116,7 +116,8 @@
         count = 2 * channels_here
         for k, ref in enumerate((tails_ref, totals_ref, heads_ref)):
             ref[:, :blocks, :] = sums[:, k * LANES : (k + 1) * LANES].reshape(count, blocks, LANES)
-            ref[:, blocks:, :] = jnp.zeros((count, SUBLANES, LANES), f32)
+            if ref.shape[1] > blocks:
+                ref[:, blocks:, :] = jnp.zeros((count, SUBLANES, LANES), f32)
 
     stacks = [jnp.zeros((lag_blocks, LANES), f32) for _ in range(templ_here)]
     for ref in framed:
@@ -185,8 +186,10 @@
             stacks[t] = stacks[t] + lags * (pick & 1).astype(f32)
 
     block_sums()
+    ahead = regrouped(0)
     for c in range(channels_here):
-        picked(c, regrouped(c), stacks)
+        ready, ahead = ahead, regrouped(c + 1) if c + 1 < channels_here else None
+        picked(c, ready, stacks)
 
     for t in range(templ_here):
         out_ref[t * lag_blocks : (t + 1) * lag_blocks, :] = stacks[t]
@@ -271,7 +274,7 @@
         scratch_shapes=[
             pltpu.SMEM(coded.shape, coded.dtype),
             pltpu.VMEM((total_rows, 2 * LANES), jnp.bfloat16),
-            pltpu.VMEM((2 * channels_here, count + SUBLANES, LANES), f32),
+            pltpu.VMEM((2 * channels_here, count, LANES), f32),
             pltpu.VMEM((2 * channels_here, count + SUBLANES, LANES), f32),
             pltpu.VMEM((2 * channels_here, count + SUBLANES, LANES), f32),
             pltpu.SemaphoreType.DMA(()),

time: 35.7 us -> 35.7 us (level)
  no operation moved by 1% of the time
where the time goes in v9:
time: 35.7 us; the launch traced here: 35.4 us
  starting transfers between devices  19 us (53%)
  waiting for transfers between devices  8.17 us (23%)
  Pallas kernels  6.46 us (18%)
  local copies, waits for them, and re-layouts  1.65 us (5%)
    ppermute x3, starting transfers between devices, swapped(): lax.ppermute(array, 'sta', [(i, i ^ distance) for i in range(lax.axis_siz...  9.83 us
    all_to_all x1, starting transfers between devices, shards(): lax.all_to_all(spread_records(records, count), 'tmpl', 0, 0, tiled=True)  9.21 us
    all_to_all x1, waiting for transfers between devices, shards(): lax.all_to_all(spread_records(records, count), 'tmpl', 0, 0, tiled=True)  4.85 us
    ppermute x3, waiting for transfers between devices, swapped(): lax.ppermute(array, 'sta', [(i, i ^ distance) for i in range(lax.axis_siz...  3.33 us
    pallas_call x1, Pallas kernels, prepared_weights(): pl.pallas_call(weights_kernel, out_shape=(jax.ShapeDtypeStruct((channels_...  2.57 us
    pallas_call x1, Pallas kernels, partial_stacks(): pl.pallas_call(lambda *refs: stack_kernel(*refs, length=length), out_shap...  2.44 us
    unnamed x3, local copies, waits for them, and re-layouts  1.65 us
    pallas_call x1, Pallas kernels, spread_records(): pl.pallas_call(spread_kernel, out_shape=jax.ShapeDtypeStruct((count * cha...  0.75 us
  transfers between devices with their start and end apart: 4, of which 4 were waited for; matrix products, arithmetic and copies ran while one was open for 3% of the time, Pallas kernels for 7%

profile of v9, /device:TPU:1, one launch (start us, length us, event | category | flops | bytes accessed | tf_op | source)
XLA Modules:
  0.0 35.4 jit_solution(16893998945468382033)
XLA Ops:
  0.0 0.0 copy-start
  0.0 0.7 %copy-done = f32[19,128]{1,0:T(8,128)S(1)} copy-done((f32[19,128]{1,0:T(8,128)S(1)}, f32[19,128]{1,0:T(8,128)}, u32[]{:S(2)}) %copy-start) | copy-done | bytes 9752
  0.7 0.7 %spread_records.1 = f32[608,128]{1,0:T(8,128)} custom-call(f32[19,128]{1,0:T(8,128)S(1)} %copy-done), custom_call_target="tpu_custom_call" | custom-call | tf_op jit(solution)/shard_map/spread_records/pallas_call | solution.py:225
  1.5 9.2 %all-to-all-start = ((f32[32,19,1,128]{3,2,1,0:T(1,128)}), f32[32,19,1,128]{3,2,1,0:T(1,128)S(1)}, u32[]{:S(2)}, u32[]{:S(2)}) async-start(f32[32,19,1,128]{3,2,1,0:T(1,128)} %bitcast.1), calls=%async_computation | async-start | bytes 622592 | tf_op jit(solution)/shard_map/all_to_all | solution.py:313
  10.7 0.9 %copy.7.templates_ref = f32[4,19,600]{2,1,0:T(8,128)S(1)} copy(f32[4,19,600]{2,0,1:T(4,128)} %param.5) | data formatting | bytes 364800 | tf_op args[1]
  11.6 2.6 %prepare_weights.1 = (bf16[19,640,128]{2,1,0:T(8,128)(2,1)S(1)}, f32[19,128]{1,0:T(8,128)S(1)}, s32[4,19]{1,0:T(4,128)S(1)}) custom-call(s32[4,19]{1,0:T(4,128)} %off_hbm.1, s32[4,19]{1,0:T(4,128)} %avail_hbm.1, f32[4,19,600]{2,1,0:T(8,128)S(1)} %copy.7.templates_ref), custom_call_target="tpu_custom_call" | custom-call | tf_op jit(solution)/shard_map/prepare_weights/pallas_call | solution.py:243
  14.2 4.8 %all-to-all-done = f32[32,19,1,128]{3,2,1,0:T(1,128)S(1)} async-done(((f32[32,19,1,128]{3,2,1,0:T(1,128)}), f32[32,19,1,128]{3,2,1,0:T(1,128)S(1)}, u32[]{:S(2)}, u32[]{:S(2)}) %all-to-all-start) | async-done | bytes 311328 | tf_op jit(solution)/shard_map/all_to_all | solution.py:313
  19.0 2.4 %stack_channels.1 = f32[96,128]{1,0:T(8,128)S(1)} custom-call(s32[4,19]{1,0:T(4,128)S(1)} %get-tuple-element.8.refs_0_, f32[19,128]{1,0:T(8,128)S(1)} %get-tuple-element.9.refs_1_, f32[608,128]{1,0:T(8,128)S(1)} %bitcast.3, bf16[19,640,128]{2,1,0:T(8,128)(2,1)S(1)} %get-tuple-element.10.refs_3_), custom_call_target="tpu_custom_call" | custom-call | tf_op jit(solution)/shard_map/stack_channels/pallas_call | solution.py:269
  21.5 2.2 %collective-permute-start = (f32[96,128]{1,0:T(8,128)S(1)}, f32[96,128]{1,0:T(8,128)S(1)}, u32[]{:S(2)}, u32[]{:S(2)}) collective-permute-start(f32[96,128]{1,0:T(8,128)S(1)} %stack_channels.1), channel_id=1, source_target_pairs={{0,1},{1,0},{2,3},{3,2},{4,5},{5,4},{6,7},{7,6},{8,9},{9,8},{10,11... | collective-permute-start | bytes 147464 | tf_op jit(solution)/shard_map/ppermute | solution.py:304
  23.7 0.9 %collective-permute-done = f32[96,128]{1,0:T(8,128)S(1)} collective-permute-done((f32[96,128]{1,0:T(8,128)S(1)}, f32[96,128]{1,0:T(8,128)S(1)}, u32[]{:S(2)}, u32[]{:S(2)}) %collective-permute-start) | collective-permute-done | bytes 49184 | tf_op jit(solution)/shard_map/ppermute | solution.py:304
  24.6 3.1 %collective-permute-start.1 = (bf16[96,128]{1,0:T(8,128)(2,1)S(1)}, bf16[96,128]{1,0:T(8,128)(2,1)S(1)}, u32[]{:S(2)}, u32[]{:S(2)}) collective-permute-start(bf16[96,128]{1,0:T(8,128)(2,1)S(1)} %get-tuple-element.13), channel_id=1, source_target_pairs={{0,2},{1,3},{2,0},{3,1},{4,6},{5,7},{6,4},{7,5},{8,10},{9,11},{10,... | collective-permute-start | bytes 73736 | tf_op jit(solution)/shard_map/ppermute | solution.py:304
  27.6 1.2 %collective-permute-done.1 = bf16[96,128]{1,0:T(8,128)(2,1)S(1)} collective-permute-done((bf16[96,128]{1,0:T(8,128)(2,1)S(1)}, bf16[96,128]{1,0:T(8,128)(2,1)S(1)}, u32[]{:S(2)}, u32[]{:S(2)}) %collective-permute-start.1) | collective-permute-done | bytes 24608 | tf_op jit(solution)/shard_map/ppermute | solution.py:304
  28.9 4.6 %collective-permute-start.2 = (bf16[96,128]{1,0:T(8,128)(2,1)S(1)}, bf16[96,128]{1,0:T(8,128)(2,1)S(1)}, u32[]{:S(2)}, u32[]{:S(2)}) collective-permute-start(bf16[96,128]{1,0:T(8,128)(2,1)S(1)} %get-tuple-element.11), channel_id=1, source_target_pairs={{0,6},{1,7},{2,4},{3,5},{4,2},{5,3},{6,0},{7,1},{8,14},{9,15},{10,... | collective-permute-start | bytes 73736 | tf_op jit(solution)/shard_map/ppermute | solution.py:304
  33.5 1.2 %collective-permute-done.2.refs_1_ = bf16[96,128]{1,0:T(8,128)(2,1)S(1)} collective-permute-done((bf16[96,128]{1,0:T(8,128)(2,1)S(1)}, bf16[96,128]{1,0:T(8,128)(2,1)S(1)}, u32[]{:S(2)}, u32[]{:S(2)}) %collective-permute-start.2) | collective-permute-done | bytes 24608 | tf_op jit(solution)/shard_map/ppermute | solution.py:304
  34.7 0.7 %finish.1 = f32[4,384]{1,0:T(4,128)} custom-call(s32[1]{0:T(128)} %bitcast.place_ref, f32[96,128]{1,0:T(8,128)S(1)} %get-tuple-element.12.refs_0_, bf16[96,128]{1,0:T(8,128)(2,1)S(1)} %collective-permute-done.2.refs_1_), custom_call_target="tpu_custom_call" | custom-call | tf_op jit(solution)/shard_map/finish/pallas_call | solution.py:289
  (2 shorter events, 0.0 us)
Async XLA Ops:
  0.0 0.7 %copy-start = (f32[19,128]{1,0:T(8,128)S(1)}, f32[19,128]{1,0:T(8,128)}, u32[]{:S(2)}) copy-start(f32[19,128]{1,0:T(8,128)} %records_ref.1) | copy-start | bytes 29188
  1.5 17.6 %all-to-all-start = ((f32[32,19,1,128]{3,2,1,0:T(1,128)}), f32[32,19,1,128]{3,2,1,0:T(1,128)S(1)}, u32[]{:S(2)}, u32[]{:S(2)}) async-start(f32[32,19,1,128]{3,2,1,0:T(1,128)} %bitcast.1), calls=%async_computation | async-start | bytes 622592 | tf_op jit(solution)/shard_map/all_to_all | solution.py:313
  21.5 3.1 %collective-permute-start = (f32[96,128]{1,0:T(8,128)S(1)}, f32[96,128]{1,0:T(8,128)S(1)}, u32[]{:S(2)}, u32[]{:S(2)}) collective-permute-start(f32[96,128]{1,0:T(8,128)S(1)} %stack_channels.1), channel_id=1, source_target_pairs={{0,1},{1,0},{2,3},{3,2},{4,5},{5,4},{6,7},{7,6},{8,9},{9,8},{10,11... | collective-permute-start | bytes 147464 | tf_op jit(solution)/shard_map/ppermute | solution.py:304
  24.6 4.3 %collective-permute-start.1 = (bf16[96,128]{1,0:T(8,128)(2,1)S(1)}, bf16[96,128]{1,0:T(8,128)(2,1)S(1)}, u32[]{:S(2)}, u32[]{:S(2)}) collective-permute-start(bf16[96,128]{1,0:T(8,128)(2,1)S(1)} %get-tuple-element.13), channel_id=1, source_target_pairs={{0,2},{1,3},{2,0},{3,1},{4,6},{5,7},{6,4},{7,5},{8,10},{9,11},{10,... | collective-permute-start | bytes 73736 | tf_op jit(solution)/shard_map/ppermute | solution.py:304
  28.9 5.8 %collective-permute-start.2 = (bf16[96,128]{1,0:T(8,128)(2,1)S(1)}, bf16[96,128]{1,0:T(8,128)(2,1)S(1)}, u32[]{:S(2)}, u32[]{:S(2)}) collective-permute-start(bf16[96,128]{1,0:T(8,128)(2,1)S(1)} %get-tuple-element.11), channel_id=1, source_target_pairs={{0,6},{1,7},{2,4},{3,5},{4,2},{5,3},{6,0},{7,1},{8,14},{9,15},{10,... | collective-permute-start | bytes 73736 | tf_op jit(solution)/shard_map/ppermute | solution.py:304
